TPU v7x, 256 devices: a whole 4x4x8 slice. The times are simulated.
256 devices in a mesh: tile: 128 (over x, y, z), rep: 2 (over core).
Axes of the slice: x: 4, y: 4, z: 8, core: 2. Of those that a mesh axis runs over, the one named last changes fastest.
Arguments:
- amplitudes: bfloat16 [2048, 128, 1024], P('tile', None, 'rep'), may hold values from -6 to 6
- integrals: bfloat16 [384, 1024, 1024], P('tile'), may hold values from -0.1875 to 0.1875
- task_cd: int32 [384], P('tile'), may hold values from 0 to 127
- task_ab: int32 [384], P('tile'), may hold values from 0 to 63
- task_allowed: int32 [384], P('tile'), may hold values from 0 to 1, as said below
- mirror: int32 [2048], P(('tile', 'rep')), may hold values from 0 to 2047, as said below
- residual_in: bfloat16 [2048, 64, 1024], P(('tile', 'rep')), may hold values from -6 to 6
Outputs:
- residual_out: bfloat16 [2048, 64, 1024], P(('tile', 'rep'))
Inputs may be any that keep to these rules, and one draw needn't show every extreme that they name: `task_allowed`: in each aligned block of 3 slots (the slots of one device along tile) one to 2 slots are allowed; some block has exactly 2. mirror is an involution on the occupied pairs without fixed points. Split the pairs into aligned blocks of 8; for b < 128, mirror maps block b one to one onto block b + 128.
All inputs are finite; a program needn't handle non-finite values.
Results may differ from a plain program's by a relative error of at most 0.0055.
Values may be sent and summed in bfloat16 or wider, within the bound.
A program may use at most 128 MiB of HBM per device.

v0:
```python
import jax
import jax.numpy as jnp
from jax import lax
from jax.sharding import PartitionSpec as P

BOTH = ("tile", "rep")


def partner_2(shard, axis, bit):
    return lax.ppermute(shard, axis, [(i, i ^ 1 << bit) for i in range(lax.axis_size(axis))])


def per_device(amplitudes, integrals, task_cd, task_ab, task_allowed, mirror, residual_in):
    peer_count = lax.axis_size("tile")
    rep_count = lax.axis_size("rep")
    rows_own, _, half_cols = amplitudes.shape
    local_rows = residual_in.shape[0]
    tile_width = integrals.shape[1]
    rep = lax.axis_index("rep")

    upper = lax.axis_index("tile") >= peer_count // 2
    partner_res = partner_2(residual_in, "tile", peer_count.bit_length() - 2)

    order = jnp.argsort(1 - task_allowed, stable=True)
    slot = order[rep]
    mine = jnp.concatenate([jnp.stack([task_cd[slot], task_ab[slot], task_allowed[slot]]), mirror])
    mine = jnp.broadcast_to(mine[None], (peer_count * rep_count, mine.shape[0]))
    every = lax.all_to_all(mine, BOTH, split_axis=0, concat_axis=0, tiled=True)
    every_cd, every_ab, every_allowed = every[:, 0], every[:, 1], every[:, 2]

    blocks = rows_own // local_rows
    own_blocks = lax.dynamic_slice_in_dim(every[:, 3:], lax.axis_index("tile") * blocks, blocks)
    inverse_rows = jnp.argsort(own_blocks % local_rows, axis=1)
    inverse_rows = (inverse_rows + local_rows * jnp.arange(blocks)[:, None]).reshape(-1)
    row_order = jnp.where(upper, inverse_rows, jnp.arange(rows_own))

    outgoing = jnp.take(jnp.take(amplitudes, row_order, axis=0), every_cd, axis=1)
    incoming = lax.all_to_all(outgoing, BOTH, split_axis=1, concat_axis=0, tiled=True)
    incoming = incoming.reshape(peer_count, rep_count, rows_own, half_cols)
    integral = lax.dynamic_index_in_dim(integrals, slot, axis=0, keepdims=False)
    integral = integral.reshape(tile_width, rep_count, half_cols)
    halves = jnp.einsum(
        "tric,arc->rtia", incoming, integral, preferred_element_type=jnp.float32
    ).astype(jnp.bfloat16)
    contribution = (halves[0].astype(jnp.float32) + halves[1].astype(jnp.float32)).astype(
        jnp.bfloat16
    )

    quarter = local_rows // 2
    pairs = contribution.reshape(2, peer_count // 2, blocks, 2, quarter, tile_width)
    pairs = pairs.transpose(3, 1, 2, 0, 4, 5).reshape(peer_count * rep_count, local_rows, tile_width)
    arrived = lax.all_to_all(pairs, BOTH, split_axis=0, concat_axis=0, tiled=True)

    tile_ids = jnp.arange(residual_in.shape[1], dtype=jnp.int32)
    weights = ((every_ab[:, None] == tile_ids[None, :]) & (every_allowed[:, None] == 1)).astype(
        jnp.bfloat16
    )
    ladder = jnp.einsum("qa,qrc->rac", weights, arrived, preferred_element_type=jnp.float32)
    ladder = ladder.reshape(2, quarter, *ladder.shape[1:])

    to_partner = mirror % local_rows
    inverse = jnp.argsort(to_partner)
    res_a = jnp.where(upper, partner_res[quarter:], residual_in[:quarter])
    res_b = jnp.where(
        upper,
        jnp.take(residual_in, inverse[quarter:], axis=0),
        jnp.take(partner_res, to_partner[:quarter], axis=0),
    )
    summed_a = res_a.astype(jnp.float32) + ladder[0]
    summed_b = res_b.astype(jnp.float32) + ladder[1]
    value = (0.5 * (summed_a - summed_b)).astype(jnp.bfloat16)
    partner_value = partner_2(value, "tile", peer_count.bit_length() - 2)
    by_lower = jnp.where(
        upper,
        jnp.concatenate([partner_value, value]),
        jnp.concatenate([value, partner_value]),
    )
    return jnp.where(upper, -jnp.take(by_lower, to_partner, axis=0), by_lower)


def solution(mesh):
    return jax.shard_map(
        per_device,
        mesh=mesh,
        in_specs=(
            P("tile", None, "rep"),
            P("tile", None, None),
            P("tile"),
            P("tile"),
            P("tile"),
            P(("tile", "rep")),
            P(("tile", "rep"), None, None),
        ),
        out_specs=P(("tile", "rep"), None, None),
        check_vma=False,
    )
```

profile of v0, /device:TPU:33, one launch (start us, length us, event | category | flops | bytes accessed | tf_op | source)
XLA Modules:
  0.0 317.4 jit_solution(13590804898426935947)
XLA Ops:
  0.0 0.0 copy-start
  0.0 0.8 broadcast_subtract_fusion
  0.8 0.7 sort.51
  1.6 0.6 dynamic_slice.19
  4.1 1.2 dynamic_slice.22
  5.3 1.2 dynamic_slice.20
  6.6 1.3 dynamic_slice.21
  7.9 2.6 pad_add_fusion
  10.5 0.7 broadcast_in_dim.50
  11.2 14.7 %all-to-all-start = ((s32[256,1,11]{2,1,0:T(1,128)}), s32[256,1,11]{2,1,0:T(1,128)S(1)}, u32[]{:S(2)}, u32[]{:S(2)}) async-start(s32[256,1,11]{2,1,0:T(1,128)} %broadcast_in_dim.50), calls=%async_computation | async-start | bytes 262144 | tf_op jit(solution)/shard_map/all_to_all | solution.py:28
  25.9 12.2 %all-to-all-done = s32[256,1,11]{2,1,0:T(1,128)S(1)} async-done(((s32[256,1,11]{2,1,0:T(1,128)}), s32[256,1,11]{2,1,0:T(1,128)S(1)}, u32[]{:S(2)}, u32[]{:S(2)}) %all-to-all-start) | async-done | bytes 11296 | tf_op jit(solution)/shard_map/all_to_all | solution.py:28
  38.2 0.1 copy.22
  38.3 0.1 add_select_fusion
  38.3 0.7 sort.52
  39.0 0.1 copy.23
  39.1 0.1 reshape.84
  39.2 0.1 reshape.83
  39.3 0.0 copy-done
  39.3 2.0 gather_fusion
  41.4 1.8 broadcast_select_fusion
  43.2 2.5 copy.25
  45.8 4.4 %gather_fusion.1 = bf16[256,16,512]{2,1,0:T(8,128)(2,1)} fusion(bf16[16,128,512]{2,0,1:T(8,128)(2,1)} %copy.25, s32[1024]{0:T(1024)S(1)} %pad_clamp_fusion.3), kind=kCustom, calls=%fused_computation.3 | custom fusion | bytes 8389632 | tf_op jit(solution)/shard_map/jit(_take)/gather | solution.py:37
  50.1 4.0 %select_bitcast_fusion = bf16[16,256,512]{2,0,1:T(8,128)(2,1)} fusion(bf16[256,16,512]{2,1,0:T(8,128)(2,1)} %gather_fusion.1, pred[256]{0:T(512)(128)(4,1)S(1)} %get-tuple-element.18), kind=kLoop, calls=%fused_computation.10 | loop fusion | flops 2097152 | bytes 8388864 | tf_op jit(solution)/shard_map/jit(_take)/select_n | solution.py:37
  54.2 8.2 %all-to-all-start.1 = ((bf16[16,256,512]{2,0,1:T(8,128)(2,1)}), bf16[16,256,512]{2,0,1:T(8,128)(2,1)}, u32[]{:S(2)}, u32[]{:S(2)}) async-start(bf16[16,256,512]{2,0,1:T(8,128)(2,1)} %select_bitcast_fusion), calls=%async_computation.1 | async-start | bytes 8388608 | tf_op jit(solution)/shard_map/all_to_all | solution.py:38
  62.4 3.1 constant_dynamic-slice_fusion
  65.5 3.9 %copy.34 = bf16[1,1024,1024]{1,2,0:T(8,128)(2,1)} copy(bf16[1,1024,1024]{2,1,0:T(8,128)(2,1)} %constant_dynamic-slice_fusion) | data formatting | bytes 4194304
  69.4 91.1 %all-to-all-done.1 = bf16[16,256,512]{2,0,1:T(8,128)(2,1)} async-done(((bf16[16,256,512]{2,0,1:T(8,128)(2,1)}), bf16[16,256,512]{2,0,1:T(8,128)(2,1)}, u32[]{:S(2)}, u32[]{:S(2)}) %all-to-all-start.1) | async-done | bytes 4194336 | tf_op jit(solution)/shard_map/all_to_all | solution.py:38
  160.5 10.4 %convolution_convert_fusion = bf16[2,128,16,1024]{3,1,2,0:T(8,128)(2,1)S(1)} fusion(bf16[1024,2,512,1]{0,2,3,1:T(8,128)(2,1)} %bitcast.28, bf16[128,2,16,512]{3,2,1,0:T(8,128)(2,1)} %bitcast.7), kind=kOutput, calls=%fused_computation.6 | convolution fusion | flops 4299161600 | bytes 14680064 | tf_op jit(solution)/shard_map/tric,arc->rtia/dot_general | solution.py:42
  170.9 2.3 add_convert_fusion
  173.2 5.2 %copy.29 = bf16[2,64,2,2,4,1024]{5,4,3,2,1,0:T(4,128)(2,1)} copy(bf16[2,64,2,2,4,1024]{5,1,3,4,0,2:T(8,128)(2,1)S(1)} %bitcast.27) | data formatting | bytes 8388608 | tf_op jit(solution)/shard_map/transpose | solution.py:51
  178.4 6.9 %reshape.87 = bf16[256,8,1024]{2,1,0:T(8,128)(2,1)} reshape(bf16[2,64,2,2,4,1024]{5,4,3,2,1,0:T(4,128)(2,1)} %copy.29) | data formatting | bytes 8388608 | tf_op jit(solution)/shard_map/reshape | solution.py:51
  185.3 7.0 %all-to-all-start.2 = ((bf16[256,8,1024]{2,1,0:T(8,128)(2,1)}), bf16[256,8,1024]{2,1,0:T(8,128)(2,1)}, u32[]{:S(2)}, u32[]{:S(2)}) async-start(bf16[256,8,1024]{2,1,0:T(8,128)(2,1)} %reshape.87), calls=%async_computation.2 | async-start | bytes 8388608 | tf_op jit(solution)/shard_map/all_to_all | solution.py:52
  192.4 2.1 collective-permute-start
  194.4 0.0 copy-done.2
  194.5 1.0 sort.53
  195.4 0.1 compare_and_fusion
  195.5 1.8 gather_fusion.3
  197.3 43.7 %collective-permute-done = bf16[8,64,1024]{2,1,0:T(8,128)(2,1)} collective-permute-done((bf16[8,64,1024]{2,1,0:T(8,128)(2,1)}, bf16[8,64,1024]{2,1,0:T(8,128)(2,1)}, u32[]{:S(2)}, u32[]{:S(2)}) %collective-permute-start) | collective-permute-done | bytes 1048608 | tf_op jit(solution)/shard_map/ppermute | solution.py:10
  241.0 2.6 gather_fusion.4
  243.6 46.1 %all-to-all-done.2 = bf16[256,8,1024]{2,1,0:T(8,128)(2,1)} async-done(((bf16[256,8,1024]{2,1,0:T(8,128)(2,1)}), bf16[256,8,1024]{2,1,0:T(8,128)(2,1)}, u32[]{:S(2)}, u32[]{:S(2)}) %all-to-all-start.2) | async-done | bytes 4194336 | tf_op jit(solution)/shard_map/all_to_all | solution.py:52
  289.7 4.8 %fusion.3 = f32[8,64,1024]{2,1,0:T(8,128)S(1)} fusion(bf16[256,8,1024]{2,1,0:T(8,128)(2,1)} %all-to-all-done.2, s32[256]{0:T(256)S(1)} %bitcast.32, pred[256]{0:T(512)(128)(4,1)S(1)} %get-tuple-element.20), kind=kOutput, calls=%fused_computation.12 | convolution fusion | flops 268468224 | bytes 6292736 | tf_op jit(solution)/shard_map/qa,qrc->rac/dot_general | solution.py:58
  294.5 0.0 copy-done.1
  294.5 1.8 fusion.8
  296.4 0.3 collective-permute-start.1
  296.7 14.2 %collective-permute-done.1 = bf16[4,64,1024]{2,1,0:T(8,128)(2,1)S(1)} collective-permute-done((bf16[4,64,1024]{2,1,0:T(8,128)(2,1)S(1)}, bf16[4,64,1024]{2,1,0:T(8,128)(2,1)S(1)}, u32[]{:S(2)}, u32[]{:S(2)}) %collective-permute-start.1) | collective-permute-done | bytes 524320 | tf_op jit(solution)/shard_map/ppermute | solution.py:10
  310.9 1.1 maximum_select_fusion
  312.0 2.8 gather_fusion.2
  314.9 2.5 negate_select_fusion
  (19 shorter events, 0.1 us)
Async XLA Ops:
  0.0 39.3 %copy-start = (bf16[16,128,512]{2,1,0:T(8,128)(2,1)S(1)}, bf16[16,128,512]{2,1,0:T(8,128)(2,1)}, u32[]{:S(2)}) copy-start(bf16[16,128,512]{2,1,0:T(8,128)(2,1)} %param.9) | copy-start | bytes 6291460
  11.2 26.9 %all-to-all-start = ((s32[256,1,11]{2,1,0:T(1,128)}), s32[256,1,11]{2,1,0:T(1,128)S(1)}, u32[]{:S(2)}, u32[]{:S(2)}) async-start(s32[256,1,11]{2,1,0:T(1,128)} %broadcast_in_dim.50), calls=%async_computation | async-start | bytes 262144 | tf_op jit(solution)/shard_map/all_to_all | solution.py:28
  54.2 106.3 %all-to-all-start.1 = ((bf16[16,256,512]{2,0,1:T(8,128)(2,1)}), bf16[16,256,512]{2,0,1:T(8,128)(2,1)}, u32[]{:S(2)}, u32[]{:S(2)}) async-start(bf16[16,256,512]{2,0,1:T(8,128)(2,1)} %select_bitcast_fusion), calls=%async_computation.1 | async-start | bytes 8388608 | tf_op jit(solution)/shard_map/all_to_all | solution.py:38
  185.3 9.1 %copy-start.2 = (s32[8]{0:T(128)S(1)}, s32[8]{0:T(128)}, u32[]{:S(2)}) copy-start(s32[8]{0:T(128)} %param.14) | copy-start | bytes 100
  185.3 104.4 %all-to-all-start.2 = ((bf16[256,8,1024]{2,1,0:T(8,128)(2,1)}), bf16[256,8,1024]{2,1,0:T(8,128)(2,1)}, u32[]{:S(2)}, u32[]{:S(2)}) async-start(bf16[256,8,1024]{2,1,0:T(8,128)(2,1)} %reshape.87), calls=%async_computation.2 | async-start | bytes 8388608 | tf_op jit(solution)/shard_map/all_to_all | solution.py:52
  192.4 48.7 %collective-permute-start = (bf16[8,64,1024]{2,1,0:T(8,128)(2,1)}, bf16[8,64,1024]{2,1,0:T(8,128)(2,1)}, u32[]{:S(2)}, u32[]{:S(2)}) collective-permute-start(bf16[8,64,1024]{2,1,0:T(8,128)(2,1)} %param.15), channel_id=1, source_target_pairs={{0,128},{2,130},{4,132},{6,134},{8,136},{10,138},{12,140},{14,142}... | collective-permute-start | bytes 3145736 | tf_op jit(solution)/shard_map/ppermute | solution.py:10
  289.7 4.8 %copy-start.1 = (bf16[4,64,1024]{2,1,0:T(8,128)(2,1)S(1)}, bf16[4,64,1024]{2,1,0:T(8,128)(2,1)}, u32[]{:S(2)}) copy-start(bf16[4,64,1024]{2,1,0:T(8,128)(2,1)} %gather_fusion.4) | copy-start | bytes 1572868
  296.4 14.5 %collective-permute-start.1 = (bf16[4,64,1024]{2,1,0:T(8,128)(2,1)S(1)}, bf16[4,64,1024]{2,1,0:T(8,128)(2,1)S(1)}, u32[]{:S(2)}, u32[]{:S(2)}) collective-permute-start(bf16[4,64,1024]{2,1,0:T(8,128)(2,1)S(1)} %fusion.8), channel_id=1, source_target_pairs={{0,128},{2,130},{4,132},{6,134},{8,136},{10,138},{12,140},{14,142}... | collective-permute-start | bytes 1572872 | tf_op jit(solution)/shard_map/ppermute | solution.py:10
where the time goes:
time: 318 us; the launch traced here: 317 us
  waiting for transfers between devices  207 us (65%)
  local copies, waits for them, and re-layouts  40.7 us (13%)
  starting transfers between devices  32.3 us (10%)
  other arithmetic  19.7 us (6%)
  matrix products  15.2 us (5%)
    all_to_all x1, waiting for transfers between devices, per_device(): lax.all_to_all(outgoing, BOTH, split_axis=1, concat_axis=0, tiled=True)  91.1 us
    ppermute x2, waiting for transfers between devices, partner_2(): lax.ppermute(shard, axis, [(i, i ^ 1 << bit) for i in range(lax.axis_size...  57.8 us
    all_to_all x1, waiting for transfers between devices, per_device(): lax.all_to_all(pairs, BOTH, split_axis=0, concat_axis=0, tiled=True)  46.1 us
    all_to_all x1, starting transfers between devices, per_device(): every = lax.all_to_all(mine, BOTH, split_axis=0, concat_axis=0, tiled=True)  14.7 us
    all_to_all x1, waiting for transfers between devices, per_device(): every = lax.all_to_all(mine, BOTH, split_axis=0, concat_axis=0, tiled=True)  12.2 us
    dot_general x1, matrix products, per_device(): jnp.einsum('tric,arc->rtia', incoming, integral, preferred_element_type=j...  10.4 us
    all_to_all x1, starting transfers between devices, per_device(): lax.all_to_all(outgoing, BOTH, split_axis=1, concat_axis=0, tiled=True)  8.24 us
    all_to_all x1, starting transfers between devices, per_device(): lax.all_to_all(pairs, BOTH, split_axis=0, concat_axis=0, tiled=True)  7.01 us
  transfers between devices with their start and end apart: 5, of which 5 were waited for; matrix products, arithmetic and copies ran while one was open for 4% of the time, Pallas kernels for 0%

commit v1 on v0

--- a/solution.py
+++ b/solution.py
@@ -48,7 +48,9 @@
 
     quarter = local_rows // 2
     pairs = contribution.reshape(2, peer_count // 2, blocks, 2, quarter, tile_width)
-    pairs = pairs.transpose(3, 1, 2, 0, 4, 5).reshape(peer_count * rep_count, local_rows, tile_width)
+    pairs = pairs[0].astype(jnp.float32) - pairs[1].astype(jnp.float32)
+    pairs = pairs.astype(jnp.bfloat16).transpose(2, 0, 1, 3, 4)
+    pairs = pairs.reshape(peer_count * rep_count, quarter, tile_width)
     arrived = lax.all_to_all(pairs, BOTH, split_axis=0, concat_axis=0, tiled=True)
 
     tile_ids = jnp.arange(residual_in.shape[1], dtype=jnp.int32)
@@ -56,7 +58,6 @@
         jnp.bfloat16
     )
     ladder = jnp.einsum("qa,qrc->rac", weights, arrived, preferred_element_type=jnp.float32)
-    ladder = ladder.reshape(2, quarter, *ladder.shape[1:])
 
     to_partner = mirror % local_rows
     inverse = jnp.argsort(to_partner)
@@ -66,9 +67,8 @@
         jnp.take(residual_in, inverse[quarter:], axis=0),
         jnp.take(partner_res, to_partner[:quarter], axis=0),
     )
-    summed_a = res_a.astype(jnp.float32) + ladder[0]
-    summed_b = res_b.astype(jnp.float32) + ladder[1]
-    value = (0.5 * (summed_a - summed_b)).astype(jnp.bfloat16)
+    diff = res_a.astype(jnp.float32) - res_b.astype(jnp.float32)
+    value = (0.5 * (diff + ladder)).astype(jnp.bfloat16)
     partner_value = partner_2(value, "tile", peer_count.bit_length() - 2)
     by_lower = jnp.where(
         upper,

time: 318 us -> 262 us (0.82)
  waiting for transfers between devices: 207 us -> 162 us
  local copies, waits for them, and re-layouts: 40.7 us -> 31.5 us
    all_to_all x1, waiting for transfers between devices: 46.1 us -> 5.95 us  [per_device(): lax.all_to_all(pairs, BOTH, split_axis=0, concat_axis=0, tiled=True)]
    reshape x1 -> x0, local copies, waits for them, and re-layouts: 6.92 us -> none  [per_device(): pairs.transpose(3, 1, 2, 0, 4, 5)]
    ppermute x2, waiting for transfers between devices: 57.8 us -> 53.1 us  [partner_2(): lax.ppermute(shard, axis, [(i, i ^ 1 << bit) for i in range(lax.axis_size...]
  transfers between devices with their start and end apart: 5 -> 5, of which waited for: 5 -> 5; matrix products, arithmetic and copies ran while one was open for 4% -> 5% of each run, Pallas kernels for 0% -> 0%
where the time goes in v1:
time: 262 us
  waiting for transfers between devices  162 us (62%)
  starting transfers between devices  32.3 us (12%)
  local copies, waits for them, and re-layouts  31.5 us (12%)
  other arithmetic  20.5 us (8%)
  matrix products  12.8 us (5%)
    all_to_all x1, waiting for transfers between devices, per_device(): lax.all_to_all(outgoing, BOTH, split_axis=1, concat_axis=0, tiled=True)  91.1 us
    ppermute x2, waiting for transfers between devices, partner_2(): lax.ppermute(shard, axis, [(i, i ^ 1 << bit) for i in range(lax.axis_size...  53.1 us
    all_to_all x1, starting transfers between devices, per_device(): every = lax.all_to_all(mine, BOTH, split_axis=0, concat_axis=0, tiled=True)  14.7 us
    all_to_all x1, waiting for transfers between devices, per_device(): every = lax.all_to_all(mine, BOTH, split_axis=0, concat_axis=0, tiled=True)  12.2 us
    dot_general x1, matrix products, per_device(): jnp.einsum('tric,arc->rtia', incoming, integral, preferred_element_type=j...  10.4 us
    all_to_all x1, starting transfers between devices, per_device(): lax.all_to_all(outgoing, BOTH, split_axis=1, concat_axis=0, tiled=True)  8.24 us
    all_to_all x1, starting transfers between devices, per_device(): lax.all_to_all(pairs, BOTH, split_axis=0, concat_axis=0, tiled=True)  7.07 us
    all_to_all x1, waiting for transfers between devices, per_device(): lax.all_to_all(pairs, BOTH, split_axis=0, concat_axis=0, tiled=True)  5.95 us
  transfers between devices with their start and end apart: 5, of which 5 were waited for; matrix products, arithmetic and copies ran while one was open for 5% of the time, Pallas kernels for 0%

profile of v1, /device:TPU:33, one launch (start us, length us, event | category | flops | bytes accessed | tf_op | source)
XLA Modules:
  0.0 261.7 jit_solution(16904642653355044843)
XLA Ops:
  0.0 0.0 copy-start
  0.0 0.8 broadcast_subtract_fusion
  0.8 0.7 sort.52
  1.6 0.6 dynamic_slice.19
  4.1 1.2 dynamic_slice.22
  5.3 1.2 dynamic_slice.20
  6.6 1.3 dynamic_slice.21
  7.9 2.6 %pad_add_fusion = s32[11]{0:T(128)S(1)} fusion(s32[8]{0:T(128)} %param.14, s32[1]{0:T(128)} %dynamic_slice.22, s32[1]{0:T(128)} %dynamic_slice.21, s32[1]{0:T(128)} %dynamic_slice.20), kind=kLoop, calls=%fused_computation.52 | loop fusion | flops 33 | bytes 88 | tf_op jit(solution)/shard_map/concatenate | solution.py:26
  10.5 0.7 broadcast_in_dim.50
  11.2 14.7 %all-to-all-start = ((s32[256,1,11]{2,1,0:T(1,128)}), s32[256,1,11]{2,1,0:T(1,128)S(1)}, u32[]{:S(2)}, u32[]{:S(2)}) async-start(s32[256,1,11]{2,1,0:T(1,128)} %broadcast_in_dim.50), calls=%async_computation | async-start | bytes 262144 | tf_op jit(solution)/shard_map/all_to_all | solution.py:28
  25.9 12.2 %all-to-all-done = s32[256,1,11]{2,1,0:T(1,128)S(1)} async-done(((s32[256,1,11]{2,1,0:T(1,128)}), s32[256,1,11]{2,1,0:T(1,128)S(1)}, u32[]{:S(2)}, u32[]{:S(2)}) %all-to-all-start) | async-done | bytes 11296 | tf_op jit(solution)/shard_map/all_to_all | solution.py:28
  38.2 0.1 copy.22
  38.3 0.1 add_select_fusion
  38.3 0.7 sort.53
  39.0 0.1 copy.23
  39.1 0.1 reshape.91
  39.2 0.1 reshape.90
  39.3 0.0 copy-done
  39.3 2.0 gather_fusion
  41.4 1.8 broadcast_select_fusion
  43.2 2.5 copy.25
  45.8 4.4 %gather_fusion.1 = bf16[256,16,512]{2,1,0:T(8,128)(2,1)} fusion(bf16[16,128,512]{2,0,1:T(8,128)(2,1)} %copy.25, s32[1024]{0:T(1024)S(1)} %pad_clamp_fusion.1), kind=kCustom, calls=%fused_computation.3 | custom fusion | bytes 8389632 | tf_op jit(solution)/shard_map/jit(_take)/gather | solution.py:37
  50.1 4.0 %select_bitcast_fusion = bf16[16,256,512]{2,0,1:T(8,128)(2,1)} fusion(bf16[256,16,512]{2,1,0:T(8,128)(2,1)} %gather_fusion.1, pred[256]{0:T(512)(128)(4,1)S(1)} %get-tuple-element.18), kind=kLoop, calls=%fused_computation.8 | loop fusion | flops 2097152 | bytes 8388864 | tf_op jit(solution)/shard_map/jit(_take)/select_n | solution.py:37
  54.2 8.2 %all-to-all-start.1 = ((bf16[16,256,512]{2,0,1:T(8,128)(2,1)}), bf16[16,256,512]{2,0,1:T(8,128)(2,1)}, u32[]{:S(2)}, u32[]{:S(2)}) async-start(bf16[16,256,512]{2,0,1:T(8,128)(2,1)} %select_bitcast_fusion), calls=%async_computation.1 | async-start | bytes 8388608 | tf_op jit(solution)/shard_map/all_to_all | solution.py:38
  62.4 3.1 %constant_dynamic-slice_fusion = bf16[1,1024,1024]{2,1,0:T(8,128)(2,1)} fusion(bf16[3,1024,1024]{2,1,0:T(8,128)(2,1)} %param.10, s32[]{:T(128)S(6)} %select_n.125), kind=kLoop, calls=%fused_computation.54 | loop fusion | bytes 4194308 | tf_op jit(solution)/shard_map/jit(dynamic_index_in_dim)/dynamic_slice | solution.py:40
  65.5 3.9 %copy.34 = bf16[1,1024,1024]{1,2,0:T(8,128)(2,1)} copy(bf16[1,1024,1024]{2,1,0:T(8,128)(2,1)} %constant_dynamic-slice_fusion) | data formatting | bytes 4194304
  69.4 91.1 %all-to-all-done.1 = bf16[16,256,512]{2,0,1:T(8,128)(2,1)} async-done(((bf16[16,256,512]{2,0,1:T(8,128)(2,1)}), bf16[16,256,512]{2,0,1:T(8,128)(2,1)}, u32[]{:S(2)}, u32[]{:S(2)}) %all-to-all-start.1) | async-done | bytes 4194336 | tf_op jit(solution)/shard_map/all_to_all | solution.py:38
  160.5 10.4 %convolution_convert_fusion = bf16[2,128,16,1024]{3,1,2,0:T(8,128)(2,1)S(1)} fusion(bf16[1024,2,512,1]{0,2,3,1:T(8,128)(2,1)} %bitcast.30, bf16[128,2,16,512]{3,2,1,0:T(8,128)(2,1)} %bitcast.7), kind=kOutput, calls=%fused_computation.6 | convolution fusion | flops 4299161600 | bytes 14680064 | tf_op jit(solution)/shard_map/tric,arc->rtia/dot_general | solution.py:42
  170.9 2.1 add_convert_fusion
  173.0 1.0 subtract_convert_fusion
  174.0 0.0 copy-start.1
  174.0 2.9 %copy.29 = bf16[2,64,2,4,1024]{4,3,2,1,0:T(4,128)(2,1)} copy(bf16[2,64,2,4,1024]{4,1,3,0,2:T(8,128)(2,1)S(1)} %bitcast.28) | data formatting | bytes 4194304 | tf_op jit(solution)/shard_map/transpose | solution.py:52
  176.9 7.1 %all-to-all-start.2 = ((bf16[256,4,1024]{2,1,0:T(4,128)(2,1)}), bf16[256,4,1024]{2,1,0:T(4,128)(2,1)}, u32[]{:S(2)}, u32[]{:S(2)}) async-start(bf16[256,4,1024]{2,1,0:T(4,128)(2,1)} %bitcast.29), calls=%async_computation.2 | async-start | bytes 4194304 | tf_op jit(solution)/shard_map/all_to_all | solution.py:54
  184.0 2.0 collective-permute-start
  186.0 0.0 copy-done.1
  186.0 1.0 sort.51
  187.0 0.1 compare_and_fusion
  187.1 1.8 gather_fusion.3
  188.9 39.0 %collective-permute-done = bf16[8,64,1024]{2,1,0:T(8,128)(2,1)} collective-permute-done((bf16[8,64,1024]{2,1,0:T(8,128)(2,1)}, bf16[8,64,1024]{2,1,0:T(8,128)(2,1)}, u32[]{:S(2)}, u32[]{:S(2)}) %collective-permute-start) | collective-permute-done | bytes 1048608 | tf_op jit(solution)/shard_map/ppermute | solution.py:10
  227.9 2.6 gather_fusion.4
  230.5 5.9 %all-to-all-done.2 = bf16[256,4,1024]{2,1,0:T(4,128)(2,1)} async-done(((bf16[256,4,1024]{2,1,0:T(4,128)(2,1)}), bf16[256,4,1024]{2,1,0:T(4,128)(2,1)}, u32[]{:S(2)}, u32[]{:S(2)}) %all-to-all-start.2) | async-done | bytes 2097184 | tf_op jit(solution)/shard_map/all_to_all | solution.py:54
  236.5 2.4 fusion.3
  238.8 1.9 multiply_convert_fusion
  240.8 0.3 collective-permute-start.1
  241.1 14.1 %collective-permute-done.1 = bf16[4,64,1024]{2,1,0:T(8,128)(2,1)S(1)} collective-permute-done((bf16[4,64,1024]{2,1,0:T(8,128)(2,1)S(1)}, bf16[4,64,1024]{2,1,0:T(8,128)(2,1)S(1)}, u32[]{:S(2)}, u32[]{:S(2)}) %collective-permute-start.1) | collective-permute-done | bytes 524320 | tf_op jit(solution)/shard_map/ppermute | solution.py:10
  255.2 1.1 maximum_select_fusion
  256.4 2.8 %gather_fusion.2 = bf16[8,64,1024]{2,1,0:T(8,128)(2,1)} fusion(bf16[8,64,1024]{2,1,0:T(8,128)(2,1)} %maximum_select_fusion, s32[1024]{0:T(1024)S(1)} %pad_clamp_fusion), kind=kCustom, calls=%fused_computation.4 | custom fusion | bytes 2097184 | tf_op jit(solution)/shard_map/jit(_take)/gather | solution.py:78
  259.2 2.5 negate_select_fusion
  (17 shorter events, 0.1 us)
Async XLA Ops:
  0.0 39.3 %copy-start = (bf16[16,128,512]{2,1,0:T(8,128)(2,1)S(1)}, bf16[16,128,512]{2,1,0:T(8,128)(2,1)}, u32[]{:S(2)}) copy-start(bf16[16,128,512]{2,1,0:T(8,128)(2,1)} %param.9) | copy-start | bytes 6291460
  11.2 26.9 %all-to-all-start = ((s32[256,1,11]{2,1,0:T(1,128)}), s32[256,1,11]{2,1,0:T(1,128)S(1)}, u32[]{:S(2)}, u32[]{:S(2)}) async-start(s32[256,1,11]{2,1,0:T(1,128)} %broadcast_in_dim.50), calls=%async_computation | async-start | bytes 262144 | tf_op jit(solution)/shard_map/all_to_all | solution.py:28
  54.2 106.3 %all-to-all-start.1 = ((bf16[16,256,512]{2,0,1:T(8,128)(2,1)}), bf16[16,256,512]{2,0,1:T(8,128)(2,1)}, u32[]{:S(2)}, u32[]{:S(2)}) async-start(bf16[16,256,512]{2,0,1:T(8,128)(2,1)} %select_bitcast_fusion), calls=%async_computation.1 | async-start | bytes 8388608 | tf_op jit(solution)/shard_map/all_to_all | solution.py:38
  174.0 12.0 %copy-start.1 = (s32[8]{0:T(128)S(1)}, s32[8]{0:T(128)}, u32[]{:S(2)}) copy-start(s32[8]{0:T(128)} %param.14) | copy-start | bytes 100
  176.9 59.5 %all-to-all-start.2 = ((bf16[256,4,1024]{2,1,0:T(4,128)(2,1)}), bf16[256,4,1024]{2,1,0:T(4,128)(2,1)}, u32[]{:S(2)}, u32[]{:S(2)}) async-start(bf16[256,4,1024]{2,1,0:T(4,128)(2,1)} %bitcast.29), calls=%async_computation.2 | async-start | bytes 4194304 | tf_op jit(solution)/shard_map/all_to_all | solution.py:54
  184.0 43.9 %collective-permute-start = (bf16[8,64,1024]{2,1,0:T(8,128)(2,1)}, bf16[8,64,1024]{2,1,0:T(8,128)(2,1)}, u32[]{:S(2)}, u32[]{:S(2)}) collective-permute-start(bf16[8,64,1024]{2,1,0:T(8,128)(2,1)} %param.15), channel_id=1, source_target_pairs={{0,128},{2,130},{4,132},{6,134},{8,136},{10,138},{12,140},{14,142}... | collective-permute-start | bytes 3145736 | tf_op jit(solution)/shard_map/ppermute | solution.py:10
  240.8 14.5 %collective-permute-start.1 = (bf16[4,64,1024]{2,1,0:T(8,128)(2,1)S(1)}, bf16[4,64,1024]{2,1,0:T(8,128)(2,1)S(1)}, u32[]{:S(2)}, u32[]{:S(2)}) collective-permute-start(bf16[4,64,1024]{2,1,0:T(8,128)(2,1)S(1)} %multiply_convert_fusion), channel_id=1, source_target_pairs={{0,128},{2,130},{4,132},{6,134},{8,136},{10,138},{12,140},{14,142}... | collective-permute-start | bytes 1572872 | tf_op jit(solution)/shard_map/ppermute | solution.py:10

commit v2 on v1

--- a/solution.py
+++ b/solution.py
@@ -37,6 +37,7 @@
     outgoing = jnp.take(jnp.take(amplitudes, row_order, axis=0), every_cd, axis=1)
     incoming = lax.all_to_all(outgoing, BOTH, split_axis=1, concat_axis=0, tiled=True)
     incoming = incoming.reshape(peer_count, rep_count, rows_own, half_cols)
+    partner_res, incoming = lax.optimization_barrier((partner_res, incoming))
     integral = lax.dynamic_index_in_dim(integrals, slot, axis=0, keepdims=False)
     integral = integral.reshape(tile_width, rep_count, half_cols)
     halves = jnp.einsum(

time: 262 us -> 260 us (level)
    all_to_all x1, waiting for transfers between devices: 91.1 us -> 49 us  [per_device(): lax.all_to_all(outgoing, BOTH, split_axis=1, concat_axis=0, tiled=True)]
    all_to_all x1, waiting for transfers between devices: 5.95 us -> 47.7 us  [per_device(): lax.all_to_all(pairs, BOTH, split_axis=0, concat_axis=0, tiled=True)]
where the time goes in v2:
time: 260 us
  waiting for transfers between devices  162 us (62%)
  starting transfers between devices  33.4 us (13%)
  local copies, waits for them, and re-layouts  30.3 us (12%)
  other arithmetic  18.2 us (7%)
  matrix products  13.3 us (5%)
    ppermute x2, waiting for transfers between devices, partner_2(): lax.ppermute(shard, axis, [(i, i ^ 1 << bit) for i in range(lax.axis_size...  53.2 us
    all_to_all x1, waiting for transfers between devices, per_device(): lax.all_to_all(outgoing, BOTH, split_axis=1, concat_axis=0, tiled=True)  49 us
    all_to_all x1, waiting for transfers between devices, per_device(): lax.all_to_all(pairs, BOTH, split_axis=0, concat_axis=0, tiled=True)  47.7 us
    all_to_all x1, starting transfers between devices, per_device(): every = lax.all_to_all(mine, BOTH, split_axis=0, concat_axis=0, tiled=True)  14.7 us
    all_to_all x1, waiting for transfers between devices, per_device(): every = lax.all_to_all(mine, BOTH, split_axis=0, concat_axis=0, tiled=True)  12.2 us
    dot_general x1, matrix products, per_device(): jnp.einsum('tric,arc->rtia', incoming, integral, preferred_element_type=j...  10.4 us
    all_to_all x1, starting transfers between devices, per_device(): lax.all_to_all(outgoing, BOTH, split_axis=1, concat_axis=0, tiled=True)  8.36 us
    all_to_all x1, starting transfers between devices, per_device(): lax.all_to_all(pairs, BOTH, split_axis=0, concat_axis=0, tiled=True)  7.07 us
  transfers between devices with their start and end apart: 5, of which 5 were waited for; matrix products, arithmetic and copies ran while one was open for 5% of the time, Pallas kernels for 0%

profile of v2, /device:TPU:33, one launch (start us, length us, event | category | flops | bytes accessed | tf_op | source)
XLA Modules:
  0.0 259.6 jit_solution(2609323603129844578)
XLA Ops:
  0.0 0.0 copy-start
  0.0 0.8 broadcast_subtract_fusion
  0.8 0.7 sort.51
  1.6 0.6 dynamic_slice.19
  4.1 1.2 dynamic_slice.22
  5.3 1.2 dynamic_slice.20
  6.6 1.3 dynamic_slice.21
  7.9 2.6 %pad_add_fusion = s32[11]{0:T(128)S(1)} fusion(s32[8]{0:T(128)} %param.14, s32[1]{0:T(128)} %dynamic_slice.22, s32[1]{0:T(128)} %dynamic_slice.21, s32[1]{0:T(128)} %dynamic_slice.20), kind=kLoop, calls=%fused_computation.53 | loop fusion | flops 33 | bytes 88 | tf_op jit(solution)/shard_map/concatenate | solution.py:26
  10.5 0.7 broadcast_in_dim.50
  11.2 14.7 %all-to-all-start = ((s32[256,1,11]{2,1,0:T(1,128)}), s32[256,1,11]{2,1,0:T(1,128)S(1)}, u32[]{:S(2)}, u32[]{:S(2)}) async-start(s32[256,1,11]{2,1,0:T(1,128)} %broadcast_in_dim.50), calls=%async_computation | async-start | bytes 262144 | tf_op jit(solution)/shard_map/all_to_all | solution.py:28
  25.9 12.2 %all-to-all-done = s32[256,1,11]{2,1,0:T(1,128)S(1)} async-done(((s32[256,1,11]{2,1,0:T(1,128)}), s32[256,1,11]{2,1,0:T(1,128)S(1)}, u32[]{:S(2)}, u32[]{:S(2)}) %all-to-all-start) | async-done | bytes 11296 | tf_op jit(solution)/shard_map/all_to_all | solution.py:28
  38.2 0.1 copy.23
  38.3 0.1 add_select_fusion
  38.3 0.7 sort.52
  39.0 0.1 copy.24
  39.1 0.1 reshape.91
  39.2 0.1 reshape.90
  39.3 0.0 copy-done
  39.3 2.0 gather_fusion
  41.4 1.8 broadcast_select_fusion
  43.2 2.5 copy.26
  45.8 4.4 %gather_fusion.1 = bf16[256,16,512]{2,1,0:T(8,128)(2,1)} fusion(bf16[16,128,512]{2,0,1:T(8,128)(2,1)} %copy.26, s32[1024]{0:T(1024)S(1)} %pad_clamp_fusion.3), kind=kCustom, calls=%fused_computation.3 | custom fusion | bytes 8389632 | tf_op jit(solution)/shard_map/jit(_take)/gather | solution.py:37
  50.1 4.0 %select_bitcast_fusion = bf16[16,256,512]{2,0,1:T(8,128)(2,1)} fusion(bf16[256,16,512]{2,1,0:T(8,128)(2,1)} %gather_fusion.1, pred[256]{0:T(512)(128)(4,1)S(1)} %get-tuple-element.22), kind=kLoop, calls=%fused_computation.8 | loop fusion | flops 2097152 | bytes 8388864 | tf_op jit(solution)/shard_map/jit(_take)/select_n | solution.py:37
  54.2 8.4 %all-to-all-start.1 = ((bf16[16,256,512]{2,0,1:T(8,128)(2,1)}), bf16[16,256,512]{2,0,1:T(8,128)(2,1)}, u32[]{:S(2)}, u32[]{:S(2)}) async-start(bf16[16,256,512]{2,0,1:T(8,128)(2,1)} %select_bitcast_fusion), calls=%async_computation.1 | async-start | bytes 8388608 | tf_op jit(solution)/shard_map/all_to_all | solution.py:38
  62.5 0.0 copy-done.3
  62.5 3.0 %collective-permute-start = (bf16[8,64,1024]{2,1,0:T(8,128)(2,1)S(1)}, bf16[8,64,1024]{2,1,0:T(8,128)(2,1)}, u32[]{:S(2)}, u32[]{:S(2)}) collective-permute-start(bf16[8,64,1024]{2,1,0:T(8,128)(2,1)S(1)} %copy-done.3), channel_id=1, source_target_pairs={{0,128},{2,130},{4,132},{6,134},{8,136},{10,138},{12,140},{14,142}... | collective-permute-start | bytes 3145736 | tf_op jit(solution)/shard_map/ppermute | solution.py:10
  65.5 3.1 %constant_dynamic-slice_fusion = bf16[1,1024,1024]{2,1,0:T(8,128)(2,1)} fusion(bf16[3,1024,1024]{2,1,0:T(8,128)(2,1)} %param.10, s32[]{:T(128)S(6)} %select_n.123), kind=kLoop, calls=%fused_computation.55 | loop fusion | bytes 4194308 | tf_op jit(solution)/shard_map/jit(dynamic_index_in_dim)/dynamic_slice | solution.py:41
  68.6 3.9 %copy.35 = bf16[1,1024,1024]{1,2,0:T(8,128)(2,1)} copy(bf16[1,1024,1024]{2,1,0:T(8,128)(2,1)} %constant_dynamic-slice_fusion) | data formatting | bytes 4194304
  72.5 39.1 %collective-permute-done = bf16[8,64,1024]{2,1,0:T(8,128)(2,1)} collective-permute-done((bf16[8,64,1024]{2,1,0:T(8,128)(2,1)S(1)}, bf16[8,64,1024]{2,1,0:T(8,128)(2,1)}, u32[]{:S(2)}, u32[]{:S(2)}) %collective-permute-start) | collective-permute-done | bytes 1048608 | tf_op jit(solution)/shard_map/ppermute | solution.py:10
  111.6 49.0 %all-to-all-done.1 = bf16[16,256,512]{2,0,1:T(8,128)(2,1)} async-done(((bf16[16,256,512]{2,0,1:T(8,128)(2,1)}), bf16[16,256,512]{2,0,1:T(8,128)(2,1)}, u32[]{:S(2)}, u32[]{:S(2)}) %all-to-all-start.1) | async-done | bytes 4194336 | tf_op jit(solution)/shard_map/all_to_all | solution.py:38
  160.6 10.4 %convolution_convert_fusion = bf16[2,128,16,1024]{3,1,2,0:T(8,128)(2,1)S(1)} fusion(bf16[1024,2,512,1]{0,2,3,1:T(8,128)(2,1)} %bitcast.36, bf16[128,2,16,512]{3,2,1,0:T(8,128)(2,1)} %bitcast.7), kind=kOutput, calls=%fused_computation.6 | convolution fusion | flops 4299161600 | bytes 14680064 | tf_op jit(solution)/shard_map/tric,arc->rtia/dot_general | solution.py:43
  171.1 2.1 add_convert_fusion
  173.1 1.0 subtract_convert_fusion
  174.1 0.0 copy-start.4
  174.1 2.9 %copy.30 = bf16[2,64,2,4,1024]{4,3,2,1,0:T(4,128)(2,1)} copy(bf16[2,64,2,4,1024]{4,1,3,0,2:T(8,128)(2,1)S(1)} %bitcast.34) | data formatting | bytes 4194304 | tf_op jit(solution)/shard_map/transpose | solution.py:53
  177.1 7.1 %all-to-all-start.2 = ((bf16[256,4,1024]{2,1,0:T(4,128)(2,1)}), bf16[256,4,1024]{2,1,0:T(4,128)(2,1)}, u32[]{:S(2)}, u32[]{:S(2)}) async-start(bf16[256,4,1024]{2,1,0:T(4,128)(2,1)} %bitcast.35), calls=%async_computation.2 | async-start | bytes 4194304 | tf_op jit(solution)/shard_map/all_to_all | solution.py:55
  184.2 1.0 sort.53
  185.1 0.1 compare_and_fusion
  185.2 1.8 gather_fusion.3
  187.1 1.8 gather_fusion.4
  188.9 47.7 %all-to-all-done.2 = bf16[256,4,1024]{2,1,0:T(4,128)(2,1)} async-done(((bf16[256,4,1024]{2,1,0:T(4,128)(2,1)}), bf16[256,4,1024]{2,1,0:T(4,128)(2,1)}, u32[]{:S(2)}, u32[]{:S(2)}) %all-to-all-start.2) | async-done | bytes 2097184 | tf_op jit(solution)/shard_map/all_to_all | solution.py:55
  236.6 2.9 %fusion.12 = bf16[4,64,1024]{2,1,0:T(8,128)(2,1)S(1)} fusion(bf16[256,4,1024]{2,1,0:T(4,128)(2,1)} %all-to-all-done.2, bf16[4,64,1024]{2,1,0:T(8,128)(2,1)S(1)} %gather_fusion.4, bf16[4,64,1024]{2,1,0:T(8,128)(2,1)S(1)} %gather_fusion.3, bf16[8,64,1024]{2,1,0:T(8,128)(2,1)} %param.15, bf16[8,64,1024]{2,1,0:T(8,128)(2,1)} %collective-permute-done, ...), kind=kOutput, calls=%fused_computation.16 | convolution fusion | flops 136871936 | bytes 4719881 | tf_op jit(solution)/shard_map/qa,qrc->rac/dot_general | solution.py:61
  239.5 0.3 collective-permute-start.1
  239.9 14.1 %collective-permute-done.1 = bf16[4,64,1024]{2,1,0:T(8,128)(2,1)S(1)} collective-permute-done((bf16[4,64,1024]{2,1,0:T(8,128)(2,1)S(1)}, bf16[4,64,1024]{2,1,0:T(8,128)(2,1)S(1)}, u32[]{:S(2)}, u32[]{:S(2)}) %collective-permute-start.1) | collective-permute-done | bytes 524320 | tf_op jit(solution)/shard_map/ppermute | solution.py:10
  254.0 0.8 copy-done.2
  254.8 0.2 maximum_select_fusion
  254.9 1.6 gather_fusion.2
  256.5 3.1 %negate_select_fusion = bf16[8,64,1024]{2,1,0:T(8,128)(2,1)} fusion(bf16[8,64,1024]{2,1,0:T(8,128)(2,1)} %gather_fusion.2, pred[8]{0:T(512)(128)(4,1)S(1)} %get-tuple-element.16, pred[]{:T(512)S(6)} %ge.27, bf16[4,64,1024]{2,1,0:T(8,128)(2,1)} %copy-done.2, bf16[4,64,1024]{2,1,0:T(8,128)(2,1)} %copy-done.1), kind=kLoop, calls=%fused_computation.18 | loop fusion | flops 3145728 | bytes 3145737 | tf_op jit(solution)/shard_map/jit(_where)/select_n | solution.py:79
  (22 shorter events, 0.1 us)
Async XLA Ops:
  0.0 39.3 %copy-start = (bf16[16,128,512]{2,1,0:T(8,128)(2,1)S(1)}, bf16[16,128,512]{2,1,0:T(8,128)(2,1)}, u32[]{:S(2)}) copy-start(bf16[16,128,512]{2,1,0:T(8,128)(2,1)} %param.9) | copy-start | bytes 6291460
  11.2 26.9 %all-to-all-start = ((s32[256,1,11]{2,1,0:T(1,128)}), s32[256,1,11]{2,1,0:T(1,128)S(1)}, u32[]{:S(2)}, u32[]{:S(2)}) async-start(s32[256,1,11]{2,1,0:T(1,128)} %broadcast_in_dim.50), calls=%async_computation | async-start | bytes 262144 | tf_op jit(solution)/shard_map/all_to_all | solution.py:28
  54.2 8.4 %copy-start.3 = (bf16[8,64,1024]{2,1,0:T(8,128)(2,1)S(1)}, bf16[8,64,1024]{2,1,0:T(8,128)(2,1)}, u32[]{:S(2)}) copy-start(bf16[8,64,1024]{2,1,0:T(8,128)(2,1)} %param.15) | copy-start | bytes 3145732
  54.2 106.5 %all-to-all-start.1 = ((bf16[16,256,512]{2,0,1:T(8,128)(2,1)}), bf16[16,256,512]{2,0,1:T(8,128)(2,1)}, u32[]{:S(2)}, u32[]{:S(2)}) async-start(bf16[16,256,512]{2,0,1:T(8,128)(2,1)} %select_bitcast_fusion), calls=%async_computation.1 | async-start | bytes 8388608 | tf_op jit(solution)/shard_map/all_to_all | solution.py:38
  62.5 49.1 %collective-permute-start = (bf16[8,64,1024]{2,1,0:T(8,128)(2,1)S(1)}, bf16[8,64,1024]{2,1,0:T(8,128)(2,1)}, u32[]{:S(2)}, u32[]{:S(2)}) collective-permute-start(bf16[8,64,1024]{2,1,0:T(8,128)(2,1)S(1)} %copy-done.3), channel_id=1, source_target_pairs={{0,128},{2,130},{4,132},{6,134},{8,136},{10,138},{12,140},{14,142}... | collective-permute-start | bytes 3145736 | tf_op jit(solution)/shard_map/ppermute | solution.py:10
  174.1 10.0 %copy-start.4 = (s32[8]{0:T(128)S(1)}, s32[8]{0:T(128)}, u32[]{:S(2)}) copy-start(s32[8]{0:T(128)} %param.14) | copy-start | bytes 100
  177.1 59.5 %all-to-all-start.2 = ((bf16[256,4,1024]{2,1,0:T(4,128)(2,1)}), bf16[256,4,1024]{2,1,0:T(4,128)(2,1)}, u32[]{:S(2)}, u32[]{:S(2)}) async-start(bf16[256,4,1024]{2,1,0:T(4,128)(2,1)} %bitcast.35), calls=%async_computation.2 | async-start | bytes 4194304 | tf_op jit(solution)/shard_map/all_to_all | solution.py:55
  239.5 14.5 %copy-start.1 = (bf16[4,64,1024]{2,1,0:T(8,128)(2,1)}, bf16[4,64,1024]{2,1,0:T(8,128)(2,1)S(1)}, u32[]{:S(2)}) copy-start(bf16[4,64,1024]{2,1,0:T(8,128)(2,1)S(1)} %fusion.12) | copy-start | bytes 1572868
  239.5 14.5 %collective-permute-start.1 = (bf16[4,64,1024]{2,1,0:T(8,128)(2,1)S(1)}, bf16[4,64,1024]{2,1,0:T(8,128)(2,1)S(1)}, u32[]{:S(2)}, u32[]{:S(2)}) collective-permute-start(bf16[4,64,1024]{2,1,0:T(8,128)(2,1)S(1)} %fusion.12), channel_id=1, source_target_pairs={{0,128},{2,130},{4,132},{6,134},{8,136},{10,138},{12,140},{14,142}... | collective-permute-start | bytes 1572872 | tf_op jit(solution)/shard_map/ppermute | solution.py:10
  254.0 0.8 copy-start.2

commit v3 on v2

--- a/solution.py
+++ b/solution.py
@@ -21,9 +21,15 @@
     upper = lax.axis_index("tile") >= peer_count // 2
     partner_res = partner_2(residual_in, "tile", peer_count.bit_length() - 2)
 
-    order = jnp.argsort(1 - task_allowed, stable=True)
-    slot = order[rep]
-    mine = jnp.concatenate([jnp.stack([task_cd[slot], task_ab[slot], task_allowed[slot]]), mirror])
+    allowed = task_allowed == 1
+    first = jnp.where(allowed[0], 0, jnp.where(allowed[1], 1, 2))
+    second = jnp.where(
+        allowed[2] & (first < 2), 2, jnp.where(allowed[1] & (first < 1), 1, (first + 1) % 3)
+    )
+    slot = jnp.where(rep == 0, first, second)
+    pick = jnp.arange(task_cd.shape[0]) == slot
+    chosen = [jnp.sum(jnp.where(pick, ids, 0)) for ids in (task_cd, task_ab, task_allowed)]
+    mine = jnp.concatenate([jnp.stack(chosen), mirror])
     mine = jnp.broadcast_to(mine[None], (peer_count * rep_count, mine.shape[0]))
     every = lax.all_to_all(mine, BOTH, split_axis=0, concat_axis=0, tiled=True)
     every_cd, every_ab, every_allowed = every[:, 0], every[:, 1], every[:, 2]
@@ -34,8 +40,9 @@
     inverse_rows = (inverse_rows + local_rows * jnp.arange(blocks)[:, None]).reshape(-1)
     row_order = jnp.where(upper, inverse_rows, jnp.arange(rows_own))
 
-    outgoing = jnp.take(jnp.take(amplitudes, row_order, axis=0), every_cd, axis=1)
-    incoming = lax.all_to_all(outgoing, BOTH, split_axis=1, concat_axis=0, tiled=True)
+    by_cd = jnp.take(amplitudes.transpose(1, 0, 2), row_order, axis=1)
+    outgoing = jnp.take(by_cd, every_cd, axis=0)
+    incoming = lax.all_to_all(outgoing, BOTH, split_axis=0, concat_axis=0, tiled=True)
     incoming = incoming.reshape(peer_count, rep_count, rows_own, half_cols)
     partner_res, incoming = lax.optimization_barrier((partner_res, incoming))
     integral = lax.dynamic_index_in_dim(integrals, slot, axis=0, keepdims=False)

time: 260 us -> 259 us (level)
  local copies, waits for them, and re-layouts: 30.3 us -> 26.6 us
    dynamic_slice x4 -> x0, local copies, waits for them, and re-layouts: 4.37 us -> none  [the longest x1 1.32 us: per_device(): task_ab[slot]]
    reduce_sum x0 -> x2, other arithmetic: none -> 2.68 us  [per_device(): jnp.sum(jnp.where(pick, ids, 0))]
where the time goes in v3:
time: 259 us
  waiting for transfers between devices  162 us (63%)
  starting transfers between devices  33.4 us (13%)
  local copies, waits for them, and re-layouts  26.6 us (10%)
  other arithmetic  20.2 us (8%)
  matrix products  13.3 us (5%)
  between operations  2.83 us (1%)
    ppermute x2, waiting for transfers between devices, partner_2(): lax.ppermute(shard, axis, [(i, i ^ 1 << bit) for i in range(lax.axis_size...  53.2 us
    all_to_all x1, waiting for transfers between devices, per_device(): lax.all_to_all(outgoing, BOTH, split_axis=0, concat_axis=0, tiled=True)  49 us
    all_to_all x1, waiting for transfers between devices, per_device(): lax.all_to_all(pairs, BOTH, split_axis=0, concat_axis=0, tiled=True)  47.7 us
    all_to_all x1, starting transfers between devices, per_device(): every = lax.all_to_all(mine, BOTH, split_axis=0, concat_axis=0, tiled=True)  14.7 us
    all_to_all x1, waiting for transfers between devices, per_device(): every = lax.all_to_all(mine, BOTH, split_axis=0, concat_axis=0, tiled=True)  12.2 us
    dot_general x1, matrix products, per_device(): jnp.einsum('tric,arc->rtia', incoming, integral, preferred_element_type=j...  10.4 us
    all_to_all x1, starting transfers between devices, per_device(): lax.all_to_all(outgoing, BOTH, split_axis=0, concat_axis=0, tiled=True)  8.36 us
    all_to_all x1, starting transfers between devices, per_device(): lax.all_to_all(pairs, BOTH, split_axis=0, concat_axis=0, tiled=True)  7.07 us
  transfers between devices with their start and end apart: 5, of which 5 were waited for; matrix products, arithmetic and copies ran while one was open for 5% of the time, Pallas kernels for 0%

profile of v3, /device:TPU:33, one launch (start us, length us, event | category | flops | bytes accessed | tf_op | source)
XLA Modules:
  0.0 258.6 jit_solution(2384620653329363561)
XLA Ops:
  0.0 0.0 copy-start
  0.0 0.8 broadcast_compare_fusion
  0.8 0.7 fusion.23
  4.1 1.4 select_reduce_fusion
  5.5 1.3 select_reduce_fusion.2
  6.8 2.6 %pad_add_fusion = s32[11]{0:T(128)S(1)} fusion(s32[8]{0:T(128)} %param.14, s32[1]{0:T(128)} %bitcast.5, s32[1]{0:T(128)} %bitcast.4, s32[1]{0:T(128)} %bitcast.3), kind=kLoop, calls=%fused_computation.53 | loop fusion | flops 33 | bytes 88 | tf_op jit(solution)/shard_map/concatenate | solution.py:32
  9.4 0.7 broadcast_in_dim.57
  10.1 14.7 %all-to-all-start = ((s32[256,1,11]{2,1,0:T(1,128)}), s32[256,1,11]{2,1,0:T(1,128)S(1)}, u32[]{:S(2)}, u32[]{:S(2)}) async-start(s32[256,1,11]{2,1,0:T(1,128)} %broadcast_in_dim.57), calls=%async_computation | async-start | bytes 262144 | tf_op jit(solution)/shard_map/all_to_all | solution.py:34
  24.8 12.2 %all-to-all-done = s32[256,1,11]{2,1,0:T(1,128)S(1)} async-done(((s32[256,1,11]{2,1,0:T(1,128)}), s32[256,1,11]{2,1,0:T(1,128)S(1)}, u32[]{:S(2)}, u32[]{:S(2)}) %all-to-all-start) | async-done | bytes 11296 | tf_op jit(solution)/shard_map/all_to_all | solution.py:34
  37.1 0.1 copy.23
  37.2 0.1 add_select_fusion
  37.3 0.7 sort.34
  37.9 0.1 copy.24
  38.0 0.1 reshape.90
  38.1 0.1 reshape.89
  38.2 0.0 copy-done
  38.2 2.0 gather_fusion
  40.3 1.8 select_bitcast_fusion
  42.1 2.5 copy.26
  44.7 4.4 %gather_fusion.1 = bf16[256,16,512]{2,1,0:T(8,128)(2,1)} fusion(bf16[128,16,512]{2,1,0:T(8,128)(2,1)} %copy.26, s32[1024]{0:T(1024)S(1)} %pad_clamp_fusion.3), kind=kCustom, calls=%fused_computation.3 | custom fusion | bytes 8389632 | tf_op jit(solution)/shard_map/jit(_take)/gather | solution.py:44
  49.0 4.0 %broadcast_select_fusion = bf16[256,16,512]{2,1,0:T(8,128)(2,1)} fusion(bf16[256,16,512]{2,1,0:T(8,128)(2,1)} %gather_fusion.1, pred[256]{0:T(512)(128)(4,1)S(1)} %get-tuple-element.20), kind=kLoop, calls=%fused_computation.9 | loop fusion | flops 2097152 | bytes 8388864 | tf_op jit(solution)/shard_map/jit(_take)/select_n | solution.py:44
  53.1 8.4 %all-to-all-start.1 = ((bf16[256,16,512]{2,1,0:T(8,128)(2,1)}), bf16[256,16,512]{2,1,0:T(8,128)(2,1)}, u32[]{:S(2)}, u32[]{:S(2)}) async-start(bf16[256,16,512]{2,1,0:T(8,128)(2,1)} %broadcast_select_fusion), calls=%async_computation.1 | async-start | bytes 8388608 | tf_op jit(solution)/shard_map/all_to_all | solution.py:45
  61.4 0.0 copy-done.3
  61.4 3.0 %collective-permute-start = (bf16[8,64,1024]{2,1,0:T(8,128)(2,1)S(1)}, bf16[8,64,1024]{2,1,0:T(8,128)(2,1)}, u32[]{:S(2)}, u32[]{:S(2)}) collective-permute-start(bf16[8,64,1024]{2,1,0:T(8,128)(2,1)S(1)} %copy-done.3), channel_id=1, source_target_pairs={{0,128},{2,130},{4,132},{6,134},{8,136},{10,138},{12,140},{14,142}... | collective-permute-start | bytes 3145736 | tf_op jit(solution)/shard_map/ppermute | solution.py:10
  64.4 3.1 %constant_dynamic-slice_fusion = bf16[1,1024,1024]{2,1,0:T(8,128)(2,1)} fusion(bf16[3,1024,1024]{2,1,0:T(8,128)(2,1)} %param.10, s32[]{:T(128)S(6)} %select_n.173), kind=kLoop, calls=%fused_computation.59 | loop fusion | bytes 4194308 | tf_op jit(solution)/shard_map/jit(dynamic_index_in_dim)/dynamic_slice | solution.py:48
  67.5 3.9 %copy.35 = bf16[1,1024,1024]{1,2,0:T(8,128)(2,1)} copy(bf16[1,1024,1024]{2,1,0:T(8,128)(2,1)} %constant_dynamic-slice_fusion) | data formatting | bytes 4194304
  71.4 39.1 %collective-permute-done = bf16[8,64,1024]{2,1,0:T(8,128)(2,1)} collective-permute-done((bf16[8,64,1024]{2,1,0:T(8,128)(2,1)S(1)}, bf16[8,64,1024]{2,1,0:T(8,128)(2,1)}, u32[]{:S(2)}, u32[]{:S(2)}) %collective-permute-start) | collective-permute-done | bytes 1048608 | tf_op jit(solution)/shard_map/ppermute | solution.py:10
  110.5 49.0 %all-to-all-done.1 = bf16[256,16,512]{2,1,0:T(8,128)(2,1)} async-done(((bf16[256,16,512]{2,1,0:T(8,128)(2,1)}), bf16[256,16,512]{2,1,0:T(8,128)(2,1)}, u32[]{:S(2)}, u32[]{:S(2)}) %all-to-all-start.1) | async-done | bytes 4194336 | tf_op jit(solution)/shard_map/all_to_all | solution.py:45
  159.5 10.4 %convolution_convert_fusion = bf16[2,128,16,1024]{3,1,2,0:T(8,128)(2,1)S(1)} fusion(bf16[1024,2,512,1]{0,2,3,1:T(8,128)(2,1)} %bitcast.39, bf16[128,2,16,512]{3,2,1,0:T(8,128)(2,1)} %bitcast.11), kind=kOutput, calls=%fused_computation.6 | convolution fusion | flops 4299161600 | bytes 14680064 | tf_op jit(solution)/shard_map/tric,arc->rtia/dot_general | solution.py:50
  170.0 2.1 add_convert_fusion
  172.0 1.0 subtract_convert_fusion
  173.0 0.0 copy-start.4
  173.1 2.9 %copy.30 = bf16[2,64,2,4,1024]{4,3,2,1,0:T(4,128)(2,1)} copy(bf16[2,64,2,4,1024]{4,1,3,0,2:T(8,128)(2,1)S(1)} %bitcast.37) | data formatting | bytes 4194304 | tf_op jit(solution)/shard_map/transpose | solution.py:60
  176.0 7.1 %all-to-all-start.2 = ((bf16[256,4,1024]{2,1,0:T(4,128)(2,1)}), bf16[256,4,1024]{2,1,0:T(4,128)(2,1)}, u32[]{:S(2)}, u32[]{:S(2)}) async-start(bf16[256,4,1024]{2,1,0:T(4,128)(2,1)} %bitcast.38), calls=%async_computation.2 | async-start | bytes 4194304 | tf_op jit(solution)/shard_map/all_to_all | solution.py:62
  183.1 0.0 copy-done.4
  183.1 1.0 sort.35
  184.1 0.1 compare_and_fusion
  184.1 1.8 gather_fusion.3
  186.0 1.8 gather_fusion.4
  187.8 47.7 %all-to-all-done.2 = bf16[256,4,1024]{2,1,0:T(4,128)(2,1)} async-done(((bf16[256,4,1024]{2,1,0:T(4,128)(2,1)}), bf16[256,4,1024]{2,1,0:T(4,128)(2,1)}, u32[]{:S(2)}, u32[]{:S(2)}) %all-to-all-start.2) | async-done | bytes 2097184 | tf_op jit(solution)/shard_map/all_to_all | solution.py:62
  235.5 2.9 %fusion.12 = bf16[4,64,1024]{2,1,0:T(8,128)(2,1)S(1)} fusion(bf16[256,4,1024]{2,1,0:T(4,128)(2,1)} %all-to-all-done.2, bf16[4,64,1024]{2,1,0:T(8,128)(2,1)S(1)} %gather_fusion.4, bf16[4,64,1024]{2,1,0:T(8,128)(2,1)S(1)} %gather_fusion.3, bf16[8,64,1024]{2,1,0:T(8,128)(2,1)} %param.15, bf16[8,64,1024]{2,1,0:T(8,128)(2,1)} %collective-permute-done, ...), kind=kOutput, calls=%fused_computation.16 | convolution fusion | flops 136871936 | bytes 4719881 | tf_op jit(solution)/shard_map/qa,qrc->rac/dot_general | solution.py:68
  238.4 0.3 collective-permute-start.1
  238.8 14.1 %collective-permute-done.1 = bf16[4,64,1024]{2,1,0:T(8,128)(2,1)S(1)} collective-permute-done((bf16[4,64,1024]{2,1,0:T(8,128)(2,1)S(1)}, bf16[4,64,1024]{2,1,0:T(8,128)(2,1)S(1)}, u32[]{:S(2)}, u32[]{:S(2)}) %collective-permute-start.1) | collective-permute-done | bytes 524320 | tf_op jit(solution)/shard_map/ppermute | solution.py:10
  252.9 0.0 copy-done.1
  252.9 0.8 copy-done.2
  253.7 0.2 maximum_select_fusion
  253.9 1.6 gather_fusion.2
  255.4 3.1 %negate_select_fusion = bf16[8,64,1024]{2,1,0:T(8,128)(2,1)} fusion(bf16[8,64,1024]{2,1,0:T(8,128)(2,1)} %gather_fusion.2, pred[8]{0:T(512)(128)(4,1)S(1)} %get-tuple-element.14, pred[]{:T(512)S(6)} %ge.27, bf16[4,64,1024]{2,1,0:T(8,128)(2,1)} %copy-done.2, bf16[4,64,1024]{2,1,0:T(8,128)(2,1)} %copy-done.1), kind=kLoop, calls=%fused_computation.18 | loop fusion | flops 3145728 | bytes 3145737 | tf_op jit(solution)/shard_map/jit(_where)/select_n | solution.py:86
  (19 shorter events, 0.1 us)
Async XLA Ops:
  0.0 38.2 %copy-start = (bf16[16,128,512]{2,1,0:T(8,128)(2,1)S(1)}, bf16[16,128,512]{2,1,0:T(8,128)(2,1)}, u32[]{:S(2)}) copy-start(bf16[16,128,512]{2,1,0:T(8,128)(2,1)} %param.9) | copy-start | bytes 6291460
  10.1 26.9 %all-to-all-start = ((s32[256,1,11]{2,1,0:T(1,128)}), s32[256,1,11]{2,1,0:T(1,128)S(1)}, u32[]{:S(2)}, u32[]{:S(2)}) async-start(s32[256,1,11]{2,1,0:T(1,128)} %broadcast_in_dim.57), calls=%async_computation | async-start | bytes 262144 | tf_op jit(solution)/shard_map/all_to_all | solution.py:34
  53.1 8.4 %copy-start.3 = (bf16[8,64,1024]{2,1,0:T(8,128)(2,1)S(1)}, bf16[8,64,1024]{2,1,0:T(8,128)(2,1)}, u32[]{:S(2)}) copy-start(bf16[8,64,1024]{2,1,0:T(8,128)(2,1)} %param.15) | copy-start | bytes 3145732
  53.1 106.5 %all-to-all-start.1 = ((bf16[256,16,512]{2,1,0:T(8,128)(2,1)}), bf16[256,16,512]{2,1,0:T(8,128)(2,1)}, u32[]{:S(2)}, u32[]{:S(2)}) async-start(bf16[256,16,512]{2,1,0:T(8,128)(2,1)} %broadcast_select_fusion), calls=%async_computation.1 | async-start | bytes 8388608 | tf_op jit(solution)/shard_map/all_to_all | solution.py:45
  61.4 49.1 %collective-permute-start = (bf16[8,64,1024]{2,1,0:T(8,128)(2,1)S(1)}, bf16[8,64,1024]{2,1,0:T(8,128)(2,1)}, u32[]{:S(2)}, u32[]{:S(2)}) collective-permute-start(bf16[8,64,1024]{2,1,0:T(8,128)(2,1)S(1)} %copy-done.3), channel_id=1, source_target_pairs={{0,128},{2,130},{4,132},{6,134},{8,136},{10,138},{12,140},{14,142}... | collective-permute-start | bytes 3145736 | tf_op jit(solution)/shard_map/ppermute | solution.py:10
  173.0 10.0 %copy-start.4 = (s32[8]{0:T(128)S(1)}, s32[8]{0:T(128)}, u32[]{:S(2)}) copy-start(s32[8]{0:T(128)} %param.14) | copy-start | bytes 100
  176.0 59.5 %all-to-all-start.2 = ((bf16[256,4,1024]{2,1,0:T(4,128)(2,1)}), bf16[256,4,1024]{2,1,0:T(4,128)(2,1)}, u32[]{:S(2)}, u32[]{:S(2)}) async-start(bf16[256,4,1024]{2,1,0:T(4,128)(2,1)} %bitcast.38), calls=%async_computation.2 | async-start | bytes 4194304 | tf_op jit(solution)/shard_map/all_to_all | solution.py:62
  238.4 14.5 %copy-start.1 = (bf16[4,64,1024]{2,1,0:T(8,128)(2,1)}, bf16[4,64,1024]{2,1,0:T(8,128)(2,1)S(1)}, u32[]{:S(2)}) copy-start(bf16[4,64,1024]{2,1,0:T(8,128)(2,1)S(1)} %fusion.12) | copy-start | bytes 1572868
  238.4 14.5 %collective-permute-start.1 = (bf16[4,64,1024]{2,1,0:T(8,128)(2,1)S(1)}, bf16[4,64,1024]{2,1,0:T(8,128)(2,1)S(1)}, u32[]{:S(2)}, u32[]{:S(2)}) collective-permute-start(bf16[4,64,1024]{2,1,0:T(8,128)(2,1)S(1)} %fusion.12), channel_id=1, source_target_pairs={{0,128},{2,130},{4,132},{6,134},{8,136},{10,138},{12,140},{14,142}... | collective-permute-start | bytes 1572872 | tf_op jit(solution)/shard_map/ppermute | solution.py:10
  252.9 0.8 copy-start.2

commit v4 on v3

--- a/solution.py
+++ b/solution.py
@@ -40,8 +40,8 @@
     inverse_rows = (inverse_rows + local_rows * jnp.arange(blocks)[:, None]).reshape(-1)
     row_order = jnp.where(upper, inverse_rows, jnp.arange(rows_own))
 
-    by_cd = jnp.take(amplitudes.transpose(1, 0, 2), row_order, axis=1)
-    outgoing = jnp.take(by_cd, every_cd, axis=0)
+    by_cd = jnp.take(amplitudes.transpose(1, 0, 2), row_order, axis=1, mode="clip")
+    outgoing = jnp.take(by_cd, every_cd, axis=0, mode="clip")
     incoming = lax.all_to_all(outgoing, BOTH, split_axis=0, concat_axis=0, tiled=True)
     incoming = incoming.reshape(peer_count, rep_count, rows_own, half_cols)
     partner_res, incoming = lax.optimization_barrier((partner_res, incoming))
@@ -72,8 +72,8 @@
     res_a = jnp.where(upper, partner_res[quarter:], residual_in[:quarter])
     res_b = jnp.where(
         upper,
-        jnp.take(residual_in, inverse[quarter:], axis=0),
-        jnp.take(partner_res, to_partner[:quarter], axis=0),
+        jnp.take(residual_in, inverse[quarter:], axis=0, mode="clip"),
+        jnp.take(partner_res, to_partner[:quarter], axis=0, mode="clip"),
     )
     diff = res_a.astype(jnp.float32) - res_b.astype(jnp.float32)
     value = (0.5 * (diff + ladder)).astype(jnp.bfloat16)
@@ -83,7 +83,7 @@
         jnp.concatenate([partner_value, value]),
         jnp.concatenate([value, partner_value]),
     )
-    return jnp.where(upper, -jnp.take(by_lower, to_partner, axis=0), by_lower)
+    return jnp.where(upper, -jnp.take(by_lower, to_partner, axis=0, mode="clip"), by_lower)
 
 
 def solution(mesh):

time: 259 us -> 255 us (0.985)
  other arithmetic: 20.2 us -> 14.1 us
    select_n x5 -> x3, other arithmetic: 8.98 us -> 3.02 us  [the longest x1 3.01 us: per_device(): jnp.where(upper, -jnp.take(by_lower, to_partner, axis=0, mode='clip'), by...]
    gather x5 -> x6, local copies, waits for them, and re-layouts: 11.6 us -> 15.6 us  [the longest x2 6.11 us: per_device(): jnp.take(amplitudes.transpose(1, 0, 2), row_order, axis=1, mode='clip')]
where the time goes in v4:
time: 255 us; the launch traced here: 254 us
  waiting for transfers between devices  162 us (64%)
  starting transfers between devices  33.4 us (13%)
  local copies, waits for them, and re-layouts  28.1 us (11%)
  other arithmetic  14.1 us (6%)
  matrix products  13.3 us (5%)
  between operations  2.8 us (1%)
    ppermute x2, waiting for transfers between devices, partner_2(): lax.ppermute(shard, axis, [(i, i ^ 1 << bit) for i in range(lax.axis_size...  53.2 us
    all_to_all x1, waiting for transfers between devices, per_device(): lax.all_to_all(outgoing, BOTH, split_axis=0, concat_axis=0, tiled=True)  49 us
    all_to_all x1, waiting for transfers between devices, per_device(): lax.all_to_all(pairs, BOTH, split_axis=0, concat_axis=0, tiled=True)  47.7 us
    all_to_all x1, starting transfers between devices, per_device(): every = lax.all_to_all(mine, BOTH, split_axis=0, concat_axis=0, tiled=True)  14.7 us
    all_to_all x1, waiting for transfers between devices, per_device(): every = lax.all_to_all(mine, BOTH, split_axis=0, concat_axis=0, tiled=True)  12.2 us
    dot_general x1, matrix products, per_device(): jnp.einsum('tric,arc->rtia', incoming, integral, preferred_element_type=j...  10.4 us
    all_to_all x1, starting transfers between devices, per_device(): lax.all_to_all(outgoing, BOTH, split_axis=0, concat_axis=0, tiled=True)  8.36 us
    all_to_all x1, starting transfers between devices, per_device(): lax.all_to_all(pairs, BOTH, split_axis=0, concat_axis=0, tiled=True)  7.07 us
  transfers between devices with their start and end apart: 5, of which 5 were waited for; matrix products, arithmetic and copies ran while one was open for 5% of the time, Pallas kernels for 0%

profile of v4, /device:TPU:33, one launch (start us, length us, event | category | flops | bytes accessed | tf_op | source)
XLA Modules:
  0.0 253.9 jit_solution(14001288910104933628)
XLA Ops:
  0.0 0.0 copy-start
  0.0 0.8 broadcast_compare_fusion
  0.8 0.7 fusion.24
  4.1 1.4 select_reduce_fusion
  5.5 1.3 select_reduce_fusion.2
  6.8 2.6 %pad_add_fusion = s32[11]{0:T(128)S(1)} fusion(s32[8]{0:T(128)} %param.12, s32[1]{0:T(128)} %bitcast.6, s32[1]{0:T(128)} %bitcast.5, s32[1]{0:T(128)} %bitcast.4), kind=kLoop, calls=%fused_computation.39 | loop fusion | flops 33 | bytes 88 | tf_op jit(solution)/shard_map/concatenate | solution.py:32
  9.4 0.7 broadcast_in_dim.30
  10.1 14.7 %all-to-all-start = ((s32[256,1,11]{2,1,0:T(1,128)}), s32[256,1,11]{2,1,0:T(1,128)S(1)}, u32[]{:S(2)}, u32[]{:S(2)}) async-start(s32[256,1,11]{2,1,0:T(1,128)} %broadcast_in_dim.30), calls=%async_computation | async-start | bytes 262144 | tf_op jit(solution)/shard_map/all_to_all | solution.py:34
  24.8 12.2 %all-to-all-done = s32[256,1,11]{2,1,0:T(1,128)S(1)} async-done(((s32[256,1,11]{2,1,0:T(1,128)}), s32[256,1,11]{2,1,0:T(1,128)S(1)}, u32[]{:S(2)}, u32[]{:S(2)}) %all-to-all-start) | async-done | bytes 11296 | tf_op jit(solution)/shard_map/all_to_all | solution.py:34
  37.1 0.1 copy.21
  37.2 0.1 add_select_fusion
  37.3 0.7 sort.34
  37.9 0.1 copy.22
  38.0 0.1 reshape.57
  38.1 0.0 copy-done
  38.1 2.0 gather_fusion
  40.1 4.1 %copy.23 = bf16[128,16,512]{2,1,0:T(8,128)(2,1)} copy(bf16[128,16,512]{2,0,1:T(8,128)(2,1)} %bitcast.39) | data formatting | bytes 4194304 | tf_op jit(solution)/shard_map/jit(_take)/gather | solution.py:43
  44.2 4.3 %gather_fusion.1 = bf16[256,16,512]{2,1,0:T(8,128)(2,1)} fusion(bf16[128,16,512]{2,1,0:T(8,128)(2,1)} %copy.23, s32[1024]{0:T(1024)S(1)} %pad_clamp_fusion.3), kind=kCustom, calls=%fused_computation.1 | custom fusion | bytes 8389632 | tf_op jit(solution)/shard_map/jit(_take)/gather | solution.py:44
  48.6 0.0 copy-start.3
  48.6 8.4 %all-to-all-start.1 = ((bf16[256,16,512]{2,1,0:T(8,128)(2,1)}), bf16[256,16,512]{2,1,0:T(8,128)(2,1)}, u32[]{:S(2)}, u32[]{:S(2)}) async-start(bf16[256,16,512]{2,1,0:T(8,128)(2,1)} %gather_fusion.1), calls=%async_computation.1 | async-start | bytes 8388608 | tf_op jit(solution)/shard_map/all_to_all | solution.py:45
  56.9 0.0 copy-done.3
  57.0 3.0 %collective-permute-start = (bf16[8,64,1024]{2,1,0:T(8,128)(2,1)S(1)}, bf16[8,64,1024]{2,1,0:T(8,128)(2,1)}, u32[]{:S(2)}, u32[]{:S(2)}) collective-permute-start(bf16[8,64,1024]{2,1,0:T(8,128)(2,1)S(1)} %copy-done.3), channel_id=1, source_target_pairs={{0,128},{2,130},{4,132},{6,134},{8,136},{10,138},{12,140},{14,142}... | collective-permute-start | bytes 3145736 | tf_op jit(solution)/shard_map/ppermute | solution.py:10
  59.9 3.1 %constant_dynamic-slice_fusion = bf16[1,1024,1024]{2,1,0:T(8,128)(2,1)} fusion(bf16[3,1024,1024]{2,1,0:T(8,128)(2,1)} %param.8, s32[]{:T(128)S(6)} %select_n.112), kind=kLoop, calls=%fused_computation.44 | loop fusion | bytes 4194308 | tf_op jit(solution)/shard_map/jit(dynamic_index_in_dim)/dynamic_slice | solution.py:48
  63.0 3.9 %copy.32 = bf16[1,1024,1024]{1,2,0:T(8,128)(2,1)} copy(bf16[1,1024,1024]{2,1,0:T(8,128)(2,1)} %constant_dynamic-slice_fusion) | data formatting | bytes 4194304
  66.9 39.1 %collective-permute-done = bf16[8,64,1024]{2,1,0:T(8,128)(2,1)} collective-permute-done((bf16[8,64,1024]{2,1,0:T(8,128)(2,1)S(1)}, bf16[8,64,1024]{2,1,0:T(8,128)(2,1)}, u32[]{:S(2)}, u32[]{:S(2)}) %collective-permute-start) | collective-permute-done | bytes 1048608 | tf_op jit(solution)/shard_map/ppermute | solution.py:10
  106.1 49.0 %all-to-all-done.1 = bf16[256,16,512]{2,1,0:T(8,128)(2,1)} async-done(((bf16[256,16,512]{2,1,0:T(8,128)(2,1)}), bf16[256,16,512]{2,1,0:T(8,128)(2,1)}, u32[]{:S(2)}, u32[]{:S(2)}) %all-to-all-start.1) | async-done | bytes 4194336 | tf_op jit(solution)/shard_map/all_to_all | solution.py:45
  155.1 10.4 %convolution_convert_fusion = bf16[2,128,16,1024]{3,1,2,0:T(8,128)(2,1)S(1)} fusion(bf16[1024,2,512,1]{0,2,3,1:T(8,128)(2,1)} %bitcast.40, bf16[128,2,16,512]{3,2,1,0:T(8,128)(2,1)} %bitcast.11), kind=kOutput, calls=%fused_computation.6 | convolution fusion | flops 4299161600 | bytes 14680064 | tf_op jit(solution)/shard_map/tric,arc->rtia/dot_general | solution.py:50
  165.5 2.1 add_convert_fusion
  167.6 1.0 subtract_convert_fusion
  168.6 0.0 copy-start.4
  168.6 2.9 %copy.27 = bf16[2,64,2,4,1024]{4,3,2,1,0:T(4,128)(2,1)} copy(bf16[2,64,2,4,1024]{4,1,3,0,2:T(8,128)(2,1)S(1)} %bitcast.37) | data formatting | bytes 4194304 | tf_op jit(solution)/shard_map/transpose | solution.py:60
  171.5 7.1 %all-to-all-start.2 = ((bf16[256,4,1024]{2,1,0:T(4,128)(2,1)}), bf16[256,4,1024]{2,1,0:T(4,128)(2,1)}, u32[]{:S(2)}, u32[]{:S(2)}) async-start(bf16[256,4,1024]{2,1,0:T(4,128)(2,1)} %bitcast.38), calls=%async_computation.2 | async-start | bytes 4194304 | tf_op jit(solution)/shard_map/all_to_all | solution.py:62
  178.6 0.0 copy-done.4
  178.6 1.0 sort.35
  179.6 0.1 slice.57
  179.6 1.8 gather_fusion.2
  181.5 1.8 gather_fusion.3
  183.3 47.7 %all-to-all-done.2 = bf16[256,4,1024]{2,1,0:T(4,128)(2,1)} async-done(((bf16[256,4,1024]{2,1,0:T(4,128)(2,1)}), bf16[256,4,1024]{2,1,0:T(4,128)(2,1)}, u32[]{:S(2)}, u32[]{:S(2)}) %all-to-all-start.2) | async-done | bytes 2097184 | tf_op jit(solution)/shard_map/all_to_all | solution.py:62
  231.0 2.9 %fusion.12 = bf16[4,64,1024]{2,1,0:T(8,128)(2,1)S(1)} fusion(bf16[256,4,1024]{2,1,0:T(4,128)(2,1)} %all-to-all-done.2, bf16[4,64,1024]{2,1,0:T(8,128)(2,1)S(1)} %gather_fusion.2, bf16[4,64,1024]{2,1,0:T(8,128)(2,1)S(1)} %gather_fusion.3, bf16[8,64,1024]{2,1,0:T(8,128)(2,1)} %param.13, bf16[8,64,1024]{2,1,0:T(8,128)(2,1)} %collective-permute-done, ...), kind=kOutput, calls=%fused_computation.14 | convolution fusion | flops 136347648 | bytes 4719873 | tf_op jit(solution)/shard_map/qa,qrc->rac/dot_general | solution.py:68
  233.9 0.0 copy-start.1
  233.9 0.3 collective-permute-start.1
  234.2 14.1 %collective-permute-done.1 = bf16[4,64,1024]{2,1,0:T(8,128)(2,1)S(1)} collective-permute-done((bf16[4,64,1024]{2,1,0:T(8,128)(2,1)S(1)}, bf16[4,64,1024]{2,1,0:T(8,128)(2,1)S(1)}, u32[]{:S(2)}, u32[]{:S(2)}) %collective-permute-start.1) | collective-permute-done | bytes 524320 | tf_op jit(solution)/shard_map/ppermute | solution.py:10
  248.4 0.0 copy-done.1
  248.4 0.0 copy-start.2
  248.4 0.8 copy-done.2
  249.2 0.2 maximum_select_fusion
  249.3 1.6 gather_fusion.4
  250.9 3.0 %negate_select_fusion = bf16[8,64,1024]{2,1,0:T(8,128)(2,1)} fusion(bf16[8,64,1024]{2,1,0:T(8,128)(2,1)} %gather_fusion.4, pred[]{:T(512)S(6)} %ge.3, bf16[4,64,1024]{2,1,0:T(8,128)(2,1)} %copy-done.2, bf16[4,64,1024]{2,1,0:T(8,128)(2,1)} %copy-done.1), kind=kLoop, calls=%fused_computation.16 | loop fusion | flops 2621440 | bytes 3145729 | tf_op jit(solution)/shard_map/jit(_where)/select_n | solution.py:86
  (14 shorter events, 0.1 us)
Async XLA Ops:
  0.0 38.1 %copy-start = (bf16[16,128,512]{2,1,0:T(8,128)(2,1)S(1)}, bf16[16,128,512]{2,1,0:T(8,128)(2,1)}, u32[]{:S(2)}) copy-start(bf16[16,128,512]{2,1,0:T(8,128)(2,1)} %param.7) | copy-start | bytes 6291460
  10.1 26.9 %all-to-all-start = ((s32[256,1,11]{2,1,0:T(1,128)}), s32[256,1,11]{2,1,0:T(1,128)S(1)}, u32[]{:S(2)}, u32[]{:S(2)}) async-start(s32[256,1,11]{2,1,0:T(1,128)} %broadcast_in_dim.30), calls=%async_computation | async-start | bytes 262144 | tf_op jit(solution)/shard_map/all_to_all | solution.py:34
  48.6 8.4 %copy-start.3 = (bf16[8,64,1024]{2,1,0:T(8,128)(2,1)S(1)}, bf16[8,64,1024]{2,1,0:T(8,128)(2,1)}, u32[]{:S(2)}) copy-start(bf16[8,64,1024]{2,1,0:T(8,128)(2,1)} %param.13) | copy-start | bytes 3145732
  48.6 106.5 %all-to-all-start.1 = ((bf16[256,16,512]{2,1,0:T(8,128)(2,1)}), bf16[256,16,512]{2,1,0:T(8,128)(2,1)}, u32[]{:S(2)}, u32[]{:S(2)}) async-start(bf16[256,16,512]{2,1,0:T(8,128)(2,1)} %gather_fusion.1), calls=%async_computation.1 | async-start | bytes 8388608 | tf_op jit(solution)/shard_map/all_to_all | solution.py:45
  57.0 49.1 %collective-permute-start = (bf16[8,64,1024]{2,1,0:T(8,128)(2,1)S(1)}, bf16[8,64,1024]{2,1,0:T(8,128)(2,1)}, u32[]{:S(2)}, u32[]{:S(2)}) collective-permute-start(bf16[8,64,1024]{2,1,0:T(8,128)(2,1)S(1)} %copy-done.3), channel_id=1, source_target_pairs={{0,128},{2,130},{4,132},{6,134},{8,136},{10,138},{12,140},{14,142}... | collective-permute-start | bytes 3145736 | tf_op jit(solution)/shard_map/ppermute | solution.py:10
  168.6 10.0 %copy-start.4 = (s32[8]{0:T(128)S(1)}, s32[8]{0:T(128)}, u32[]{:S(2)}) copy-start(s32[8]{0:T(128)} %param.12) | copy-start | bytes 100
  171.5 59.5 %all-to-all-start.2 = ((bf16[256,4,1024]{2,1,0:T(4,128)(2,1)}), bf16[256,4,1024]{2,1,0:T(4,128)(2,1)}, u32[]{:S(2)}, u32[]{:S(2)}) async-start(bf16[256,4,1024]{2,1,0:T(4,128)(2,1)} %bitcast.38), calls=%async_computation.2 | async-start | bytes 4194304 | tf_op jit(solution)/shard_map/all_to_all | solution.py:62
  233.9 14.5 %copy-start.1 = (bf16[4,64,1024]{2,1,0:T(8,128)(2,1)}, bf16[4,64,1024]{2,1,0:T(8,128)(2,1)S(1)}, u32[]{:S(2)}) copy-start(bf16[4,64,1024]{2,1,0:T(8,128)(2,1)S(1)} %fusion.12) | copy-start | bytes 1572868
  233.9 14.5 %collective-permute-start.1 = (bf16[4,64,1024]{2,1,0:T(8,128)(2,1)S(1)}, bf16[4,64,1024]{2,1,0:T(8,128)(2,1)S(1)}, u32[]{:S(2)}, u32[]{:S(2)}) collective-permute-start(bf16[4,64,1024]{2,1,0:T(8,128)(2,1)S(1)} %fusion.12), channel_id=1, source_target_pairs={{0,128},{2,130},{4,132},{6,134},{8,136},{10,138},{12,140},{14,142}... | collective-permute-start | bytes 1572872 | tf_op jit(solution)/shard_map/ppermute | solution.py:10
  248.4 0.8 copy-start.2

commit v5 on v4

--- a/solution.py
+++ b/solution.py
@@ -40,8 +40,7 @@
     inverse_rows = (inverse_rows + local_rows * jnp.arange(blocks)[:, None]).reshape(-1)
     row_order = jnp.where(upper, inverse_rows, jnp.arange(rows_own))
 
-    by_cd = jnp.take(amplitudes.transpose(1, 0, 2), row_order, axis=1, mode="clip")
-    outgoing = jnp.take(by_cd, every_cd, axis=0, mode="clip")
+    outgoing = amplitudes.at[row_order[None, :], every_cd[:, None]].get(mode="clip")
     incoming = lax.all_to_all(outgoing, BOTH, split_axis=0, concat_axis=0, tiled=True)
     incoming = incoming.reshape(peer_count, rep_count, rows_own, half_cols)
     partner_res, incoming = lax.optimization_barrier((partner_res, incoming))
@@ -78,12 +77,12 @@
     diff = res_a.astype(jnp.float32) - res_b.astype(jnp.float32)
     value = (0.5 * (diff + ladder)).astype(jnp.bfloat16)
     partner_value = partner_2(value, "tile", peer_count.bit_length() - 2)
-    by_lower = jnp.where(
-        upper,
-        jnp.concatenate([partner_value, value]),
-        jnp.concatenate([value, partner_value]),
+    by_lower = jnp.concatenate(
+        [jnp.where(upper, partner_value, value), jnp.where(upper, value, partner_value)]
     )
-    return jnp.where(upper, -jnp.take(by_lower, to_partner, axis=0, mode="clip"), by_lower)
+    place = jnp.where(upper, to_partner, jnp.arange(local_rows))
+    sign = jnp.where(upper, -1.0, 1.0).astype(jnp.bfloat16)
+    return sign * jnp.take(by_lower, place, axis=0, mode="clip")
 
 
 def solution(mesh):

time: 255 us -> 290 us (1.14)
  local copies, waits for them, and re-layouts: 28.1 us -> 65.4 us
    gather x4 -> x2, local copies, waits for them, and re-layouts: 12 us -> 49.2 us  [the longest x1 47.4 us: per_device(): amplitudes.at[row_order[None, :], every_cd[:, None]].get(mode='clip')]
    select_n x4 -> x2, other arithmetic: 3.19 us -> 0.08 us  [the longest x1 0.07 us: per_device(): jnp.where(upper, partner_value, value)]
  transfers between devices with their start and end apart: 5 -> 5, of which waited for: 5 -> 5; matrix products, arithmetic and copies ran while one was open for 5% -> 4% of each run, Pallas kernels for 0% -> 0%
where the time goes in v5:
time: 290 us
  waiting for transfers between devices  161 us (56%)
  local copies, waits for them, and re-layouts  65.4 us (23%)
  starting transfers between devices  33.4 us (12%)
  matrix products  13.5 us (5%)
  other arithmetic  13.2 us (5%)
    ppermute x2, waiting for transfers between devices, partner_2(): lax.ppermute(shard, axis, [(i, i ^ 1 << bit) for i in range(lax.axis_size...  53.4 us
    all_to_all x1, waiting for transfers between devices, per_device(): lax.all_to_all(outgoing, BOTH, split_axis=0, concat_axis=0, tiled=True)  49 us
    gather x1, local copies, waits for them, and re-layouts, per_device(): amplitudes.at[row_order[None, :], every_cd[:, None]].get(mode='clip')  47.4 us
    all_to_all x1, waiting for transfers between devices, per_device(): lax.all_to_all(pairs, BOTH, split_axis=0, concat_axis=0, tiled=True)  46.8 us
    all_to_all x1, starting transfers between devices, per_device(): every = lax.all_to_all(mine, BOTH, split_axis=0, concat_axis=0, tiled=True)  14.7 us
    all_to_all x1, waiting for transfers between devices, per_device(): every = lax.all_to_all(mine, BOTH, split_axis=0, concat_axis=0, tiled=True)  12.2 us
    dot_general x1, matrix products, per_device(): jnp.einsum('tric,arc->rtia', incoming, integral, preferred_element_type=j...  10.4 us
    all_to_all x1, starting transfers between devices, per_device(): lax.all_to_all(outgoing, BOTH, split_axis=0, concat_axis=0, tiled=True)  8.36 us
  transfers between devices with their start and end apart: 5, of which 5 were waited for; matrix products, arithmetic and copies ran while one was open for 4% of the time, Pallas kernels for 0%

profile of v5, /device:TPU:33, one launch (start us, length us, event | category | flops | bytes accessed | tf_op | source)
XLA Modules:
  0.0 289.7 jit_solution(11172405567545587992)
XLA Ops:
  0.0 0.0 copy-start
  0.0 0.8 broadcast_compare_fusion
  0.8 0.7 fusion.25
  4.1 1.4 select_reduce_fusion
  5.5 1.3 select_reduce_fusion.2
  6.8 2.6 pad_add_fusion
  9.4 0.7 broadcast_in_dim.37
  10.1 14.7 %all-to-all-start = ((s32[256,1,11]{2,1,0:T(1,128)}), s32[256,1,11]{2,1,0:T(1,128)S(1)}, u32[]{:S(2)}, u32[]{:S(2)}) async-start(s32[256,1,11]{2,1,0:T(1,128)} %broadcast_in_dim.37), calls=%async_computation | async-start | bytes 262144 | tf_op jit(solution)/shard_map/all_to_all | solution.py:34
  24.8 12.2 %all-to-all-done = s32[256,1,11]{2,1,0:T(1,128)S(1)} async-done(((s32[256,1,11]{2,1,0:T(1,128)}), s32[256,1,11]{2,1,0:T(1,128)S(1)}, u32[]{:S(2)}, u32[]{:S(2)}) %all-to-all-start) | async-done | bytes 11296 | tf_op jit(solution)/shard_map/all_to_all | solution.py:34
  37.1 0.1 copy.14
  37.2 0.1 add_select_fusion
  37.3 0.7 sort.34
  37.9 0.1 copy.15
  38.0 0.1 reshape.57
  38.1 0.1 broadcast_or_fusion
  38.2 0.1 reshape.66
  38.3 0.0 copy-done
  38.3 47.4 %gather_fusion = bf16[4096,512]{1,0:T(8,128)(2,1)} fusion(bf16[16,128,512]{2,1,0:T(8,128)(2,1)S(1)} %copy-done, s32[4096]{0:T(1024)S(1)} %reshape.66), kind=kCustom, calls=%fused_computation | custom fusion | bytes 8421376 | tf_op jit(solution)/shard_map/gather | solution.py:43
  85.7 0.0 copy-start.1
  85.7 8.4 %all-to-all-start.1 = ((bf16[256,16,512]{2,1,0:T(8,128)(2,1)}), bf16[256,16,512]{2,1,0:T(8,128)(2,1)}, u32[]{:S(2)}, u32[]{:S(2)}) async-start(bf16[256,16,512]{2,1,0:T(8,128)(2,1)} %bitcast.35), calls=%async_computation.1 | async-start | bytes 8388608 | tf_op jit(solution)/shard_map/all_to_all | solution.py:44
  94.1 0.0 copy-done.1
  94.1 3.0 %collective-permute-start = (bf16[8,64,1024]{2,1,0:T(8,128)(2,1)S(1)}, bf16[8,64,1024]{2,1,0:T(8,128)(2,1)}, u32[]{:S(2)}, u32[]{:S(2)}) collective-permute-start(bf16[8,64,1024]{2,1,0:T(8,128)(2,1)S(1)} %copy-done.1), channel_id=1, source_target_pairs={{0,128},{2,130},{4,132},{6,134},{8,136},{10,138},{12,140},{14,142}... | collective-permute-start | bytes 3145736 | tf_op jit(solution)/shard_map/ppermute | solution.py:10
  97.1 3.1 %constant_dynamic-slice_fusion = bf16[1,1024,1024]{2,1,0:T(8,128)(2,1)} fusion(bf16[3,1024,1024]{2,1,0:T(8,128)(2,1)} %param.8, s32[]{:T(128)S(6)} %select_n.131), kind=kLoop, calls=%fused_computation.49 | loop fusion | bytes 4194308 | tf_op jit(solution)/shard_map/jit(dynamic_index_in_dim)/dynamic_slice | solution.py:47
  100.1 3.9 %copy.24 = bf16[1,1024,1024]{1,2,0:T(8,128)(2,1)} copy(bf16[1,1024,1024]{2,1,0:T(8,128)(2,1)} %constant_dynamic-slice_fusion) | data formatting | bytes 4194304
  104.1 39.1 %collective-permute-done = bf16[8,64,1024]{2,1,0:T(8,128)(2,1)} collective-permute-done((bf16[8,64,1024]{2,1,0:T(8,128)(2,1)S(1)}, bf16[8,64,1024]{2,1,0:T(8,128)(2,1)}, u32[]{:S(2)}, u32[]{:S(2)}) %collective-permute-start) | collective-permute-done | bytes 1048608 | tf_op jit(solution)/shard_map/ppermute | solution.py:10
  143.2 49.0 %all-to-all-done.1 = bf16[256,16,512]{2,1,0:T(8,128)(2,1)} async-done(((bf16[256,16,512]{2,1,0:T(8,128)(2,1)}), bf16[256,16,512]{2,1,0:T(8,128)(2,1)}, u32[]{:S(2)}, u32[]{:S(2)}) %all-to-all-start.1) | async-done | bytes 4194336 | tf_op jit(solution)/shard_map/all_to_all | solution.py:44
  192.2 10.4 %convolution_convert_fusion = bf16[2,128,16,1024]{3,1,2,0:T(8,128)(2,1)S(1)} fusion(bf16[1024,2,512,1]{0,2,3,1:T(8,128)(2,1)} %bitcast.38, bf16[128,2,16,512]{3,2,1,0:T(8,128)(2,1)} %bitcast.9), kind=kOutput, calls=%fused_computation.5 | convolution fusion | flops 4299161600 | bytes 14680064 | tf_op jit(solution)/shard_map/tric,arc->rtia/dot_general | solution.py:49
  202.6 2.1 add_convert_fusion
  204.7 1.0 subtract_convert_fusion
  205.7 2.9 %copy.19 = bf16[2,64,2,4,1024]{4,3,2,1,0:T(4,128)(2,1)} copy(bf16[2,64,2,4,1024]{4,1,3,0,2:T(8,128)(2,1)S(1)} %bitcast.36) | data formatting | bytes 4194304 | tf_op jit(solution)/shard_map/transpose | solution.py:59
  208.6 0.0 copy-start.2
  208.6 7.2 %all-to-all-start.2 = ((bf16[256,4,1024]{2,1,0:T(4,128)(2,1)}), bf16[256,4,1024]{2,1,0:T(4,128)(2,1)}, u32[]{:S(2)}, u32[]{:S(2)}) async-start(bf16[256,4,1024]{2,1,0:T(4,128)(2,1)} %bitcast.37), calls=%async_computation.2 | async-start | bytes 4194304 | tf_op jit(solution)/shard_map/all_to_all | solution.py:61
  215.8 0.0 copy-done.2
  215.9 1.0 sort.35
  216.8 0.1 slice.57
  216.9 1.8 gather_fusion.1
  218.8 2.6 gather_fusion.2
  221.4 46.8 %all-to-all-done.2 = bf16[256,4,1024]{2,1,0:T(4,128)(2,1)} async-done(((bf16[256,4,1024]{2,1,0:T(4,128)(2,1)}), bf16[256,4,1024]{2,1,0:T(4,128)(2,1)}, u32[]{:S(2)}, u32[]{:S(2)}) %all-to-all-start.2) | async-done | bytes 2097184 | tf_op jit(solution)/shard_map/all_to_all | solution.py:61
  268.1 3.0 %fusion.12 = bf16[4,64,1024]{2,1,0:T(8,128)(2,1)S(1)} fusion(bf16[256,4,1024]{2,1,0:T(4,128)(2,1)} %all-to-all-done.2, bf16[4,64,1024]{2,1,0:T(8,128)(2,1)S(1)} %gather_fusion.1, bf16[4,64,1024]{2,1,0:T(8,128)(2,1)} %gather_fusion.2, bf16[8,64,1024]{2,1,0:T(8,128)(2,1)} %param.13, bf16[8,64,1024]{2,1,0:T(8,128)(2,1)} %collective-permute-done, pred[]{:T(512)S(6)} %ge.3, ...), kind=kOutput, calls=%fused_computation.13 | convolution fusion | flops 136347648 | bytes 4719873 | tf_op jit(solution)/shard_map/qa,qrc->rac/dot_general | solution.py:67
  271.2 0.2 collective-permute-start.1
  271.4 14.3 %collective-permute-done.1 = bf16[4,64,1024]{2,1,0:T(8,128)(2,1)S(1)} collective-permute-done((bf16[4,64,1024]{2,1,0:T(8,128)(2,1)S(1)}, bf16[4,64,1024]{2,1,0:T(8,128)(2,1)S(1)}, u32[]{:S(2)}, u32[]{:S(2)}) %collective-permute-start.1) | collective-permute-done | bytes 524320 | tf_op jit(solution)/shard_map/ppermute | solution.py:10
  285.6 0.1 broadcast_select_fusion
  285.7 1.1 pad_maximum_fusion
  286.8 1.8 gather_fusion.3
  288.6 1.0 broadcast_multiply_fusion
  (12 shorter events, 0.1 us)
Async XLA Ops:
  0.0 38.3 %copy-start = (bf16[16,128,512]{2,1,0:T(8,128)(2,1)S(1)}, bf16[16,128,512]{2,1,0:T(8,128)(2,1)}, u32[]{:S(2)}) copy-start(bf16[16,128,512]{2,1,0:T(8,128)(2,1)} %param.7) | copy-start | bytes 6291460
  10.1 26.9 %all-to-all-start = ((s32[256,1,11]{2,1,0:T(1,128)}), s32[256,1,11]{2,1,0:T(1,128)S(1)}, u32[]{:S(2)}, u32[]{:S(2)}) async-start(s32[256,1,11]{2,1,0:T(1,128)} %broadcast_in_dim.37), calls=%async_computation | async-start | bytes 262144 | tf_op jit(solution)/shard_map/all_to_all | solution.py:34
  85.7 8.4 %copy-start.1 = (bf16[8,64,1024]{2,1,0:T(8,128)(2,1)S(1)}, bf16[8,64,1024]{2,1,0:T(8,128)(2,1)}, u32[]{:S(2)}) copy-start(bf16[8,64,1024]{2,1,0:T(8,128)(2,1)} %param.13) | copy-start | bytes 3145732
  85.7 106.5 %all-to-all-start.1 = ((bf16[256,16,512]{2,1,0:T(8,128)(2,1)}), bf16[256,16,512]{2,1,0:T(8,128)(2,1)}, u32[]{:S(2)}, u32[]{:S(2)}) async-start(bf16[256,16,512]{2,1,0:T(8,128)(2,1)} %bitcast.35), calls=%async_computation.1 | async-start | bytes 8388608 | tf_op jit(solution)/shard_map/all_to_all | solution.py:44
  94.1 49.1 %collective-permute-start = (bf16[8,64,1024]{2,1,0:T(8,128)(2,1)S(1)}, bf16[8,64,1024]{2,1,0:T(8,128)(2,1)}, u32[]{:S(2)}, u32[]{:S(2)}) collective-permute-start(bf16[8,64,1024]{2,1,0:T(8,128)(2,1)S(1)} %copy-done.1), channel_id=1, source_target_pairs={{0,128},{2,130},{4,132},{6,134},{8,136},{10,138},{12,140},{14,142}... | collective-permute-start | bytes 3145736 | tf_op jit(solution)/shard_map/ppermute | solution.py:10
  208.6 7.2 %copy-start.2 = (s32[8]{0:T(128)S(1)}, s32[8]{0:T(128)}, u32[]{:S(2)}) copy-start(s32[8]{0:T(128)} %param.12) | copy-start | bytes 100
  208.6 59.5 %all-to-all-start.2 = ((bf16[256,4,1024]{2,1,0:T(4,128)(2,1)}), bf16[256,4,1024]{2,1,0:T(4,128)(2,1)}, u32[]{:S(2)}, u32[]{:S(2)}) async-start(bf16[256,4,1024]{2,1,0:T(4,128)(2,1)} %bitcast.37), calls=%async_computation.2 | async-start | bytes 4194304 | tf_op jit(solution)/shard_map/all_to_all | solution.py:61
  271.2 14.5 %collective-permute-start.1 = (bf16[4,64,1024]{2,1,0:T(8,128)(2,1)S(1)}, bf16[4,64,1024]{2,1,0:T(8,128)(2,1)S(1)}, u32[]{:S(2)}, u32[]{:S(2)}) collective-permute-start(bf16[4,64,1024]{2,1,0:T(8,128)(2,1)S(1)} %fusion.12), channel_id=1, source_target_pairs={{0,128},{2,130},{4,132},{6,134},{8,136},{10,138},{12,140},{14,142}... | collective-permute-start | bytes 1572872 | tf_op jit(solution)/shard_map/ppermute | solution.py:10

commit v6 on v5

--- a/solution.py
+++ b/solution.py
@@ -40,8 +40,9 @@
     inverse_rows = (inverse_rows + local_rows * jnp.arange(blocks)[:, None]).reshape(-1)
     row_order = jnp.where(upper, inverse_rows, jnp.arange(rows_own))
 
-    outgoing = amplitudes.at[row_order[None, :], every_cd[:, None]].get(mode="clip")
-    incoming = lax.all_to_all(outgoing, BOTH, split_axis=0, concat_axis=0, tiled=True)
+    by_row = jnp.take(amplitudes, row_order, axis=0, mode="clip")
+    outgoing = jnp.take(by_row, every_cd, axis=1, mode="clip")
+    incoming = lax.all_to_all(outgoing, BOTH, split_axis=1, concat_axis=0, tiled=True)
     incoming = incoming.reshape(peer_count, rep_count, rows_own, half_cols)
     partner_res, incoming = lax.optimization_barrier((partner_res, incoming))
     integral = lax.dynamic_index_in_dim(integrals, slot, axis=0, keepdims=False)

time: 290 us -> 253 us (0.87)
  local copies, waits for them, and re-layouts: 65.4 us -> 28.3 us
    gather x1 -> x3, local copies, waits for them, and re-layouts: 47.4 us -> 10.5 us  [the longest x2 6.11 us: per_device(): by_row = jnp.take(amplitudes, row_order, axis=0, mode='clip')]
  transfers between devices with their start and end apart: 5 -> 5, of which waited for: 5 -> 5; matrix products, arithmetic and copies ran while one was open for 4% -> 5% of each run, Pallas kernels for 0% -> 0%
where the time goes in v6:
time: 253 us
  waiting for transfers between devices  162 us (64%)
  starting transfers between devices  33.3 us (13%)
  local copies, waits for them, and re-layouts  28.3 us (11%)
  matrix products  13.4 us (5%)
  other arithmetic  13.1 us (5%)
  between operations  2.79 us (1%)
    ppermute x2, waiting for transfers between devices, partner_2(): lax.ppermute(shard, axis, [(i, i ^ 1 << bit) for i in range(lax.axis_size...  53.4 us
    all_to_all x1, waiting for transfers between devices, per_device(): lax.all_to_all(outgoing, BOTH, split_axis=1, concat_axis=0, tiled=True)  49 us
    all_to_all x1, waiting for transfers between devices, per_device(): lax.all_to_all(pairs, BOTH, split_axis=0, concat_axis=0, tiled=True)  46.9 us
    all_to_all x1, starting transfers between devices, per_device(): every = lax.all_to_all(mine, BOTH, split_axis=0, concat_axis=0, tiled=True)  14.7 us
    all_to_all x1, waiting for transfers between devices, per_device(): every = lax.all_to_all(mine, BOTH, split_axis=0, concat_axis=0, tiled=True)  12.2 us
    dot_general x1, matrix products, per_device(): jnp.einsum('tric,arc->rtia', incoming, integral, preferred_element_type=j...  10.4 us
    all_to_all x1, starting transfers between devices, per_device(): lax.all_to_all(outgoing, BOTH, split_axis=1, concat_axis=0, tiled=True)  8.36 us
    all_to_all x1, starting transfers between devices, per_device(): lax.all_to_all(pairs, BOTH, split_axis=0, concat_axis=0, tiled=True)  7.07 us
  transfers between devices with their start and end apart: 5, of which 5 were waited for; matrix products, arithmetic and copies ran while one was open for 5% of the time, Pallas kernels for 0%

profile of v6, /device:TPU:33, one launch (start us, length us, event | category | flops | bytes accessed | tf_op | source)
XLA Modules:
  0.0 252.5 jit_solution(15138187195903246469)
XLA Ops:
  0.0 0.0 copy-start
  0.0 0.8 broadcast_compare_fusion
  0.8 0.7 fusion.24
  4.1 1.4 select_reduce_fusion
  5.5 1.3 select_reduce_fusion.2
  6.8 2.6 %pad_add_fusion = s32[11]{0:T(128)S(1)} fusion(s32[8]{0:T(128)} %param.12, s32[1]{0:T(128)} %bitcast.5, s32[1]{0:T(128)} %bitcast.4, s32[1]{0:T(128)} %bitcast.3), kind=kLoop, calls=%fused_computation.42 | loop fusion | flops 33 | bytes 88 | tf_op jit(solution)/shard_map/concatenate | solution.py:32
  9.4 0.7 broadcast_in_dim.30
  10.1 14.7 %all-to-all-start = ((s32[256,1,11]{2,1,0:T(1,128)}), s32[256,1,11]{2,1,0:T(1,128)S(1)}, u32[]{:S(2)}, u32[]{:S(2)}) async-start(s32[256,1,11]{2,1,0:T(1,128)} %broadcast_in_dim.30), calls=%async_computation | async-start | bytes 262144 | tf_op jit(solution)/shard_map/all_to_all | solution.py:34
  24.8 12.2 %all-to-all-done = s32[256,1,11]{2,1,0:T(1,128)S(1)} async-done(((s32[256,1,11]{2,1,0:T(1,128)}), s32[256,1,11]{2,1,0:T(1,128)S(1)}, u32[]{:S(2)}, u32[]{:S(2)}) %all-to-all-start) | async-done | bytes 11296 | tf_op jit(solution)/shard_map/all_to_all | solution.py:34
  37.1 0.1 copy.21
  37.2 0.1 add_select_fusion
  37.3 0.7 sort.34
  37.9 0.1 copy.22
  38.0 0.1 reshape.58
  38.1 0.0 copy-done
  38.1 2.0 gather_fusion
  40.1 4.1 %copy.23 = bf16[16,128,512]{2,0,1:T(8,128)(2,1)} copy(bf16[16,128,512]{2,1,0:T(8,128)(2,1)} %gather_fusion) | data formatting | bytes 4194304 | tf_op jit(solution)/shard_map/jit(_take)/gather | solution.py:43
  44.2 4.3 %gather_fusion.1 = bf16[256,16,512]{2,1,0:T(8,128)(2,1)} fusion(bf16[16,128,512]{2,0,1:T(8,128)(2,1)} %copy.23, s32[1024]{0:T(1024)S(1)} %pad_clamp_fusion.3), kind=kCustom, calls=%fused_computation.1 | custom fusion | bytes 8389632 | tf_op jit(solution)/shard_map/jit(_take)/gather | solution.py:44
  48.6 0.0 copy-start.1
  48.6 8.4 %all-to-all-start.1 = ((bf16[16,256,512]{2,0,1:T(8,128)(2,1)}), bf16[16,256,512]{2,0,1:T(8,128)(2,1)}, u32[]{:S(2)}, u32[]{:S(2)}) async-start(bf16[16,256,512]{2,0,1:T(8,128)(2,1)} %bitcast.39), calls=%async_computation.1 | async-start | bytes 8388608 | tf_op jit(solution)/shard_map/all_to_all | solution.py:45
  56.9 0.0 copy-done.1
  57.0 3.0 %collective-permute-start = (bf16[8,64,1024]{2,1,0:T(8,128)(2,1)S(1)}, bf16[8,64,1024]{2,1,0:T(8,128)(2,1)}, u32[]{:S(2)}, u32[]{:S(2)}) collective-permute-start(bf16[8,64,1024]{2,1,0:T(8,128)(2,1)S(1)} %copy-done.1), channel_id=1, source_target_pairs={{0,128},{2,130},{4,132},{6,134},{8,136},{10,138},{12,140},{14,142}... | collective-permute-start | bytes 3145736 | tf_op jit(solution)/shard_map/ppermute | solution.py:10
  59.9 3.1 %constant_dynamic-slice_fusion = bf16[1,1024,1024]{2,1,0:T(8,128)(2,1)} fusion(bf16[3,1024,1024]{2,1,0:T(8,128)(2,1)} %param.8, s32[]{:T(128)S(6)} %select_n.120), kind=kLoop, calls=%fused_computation.47 | loop fusion | bytes 4194308 | tf_op jit(solution)/shard_map/jit(dynamic_index_in_dim)/dynamic_slice | solution.py:48
  63.0 3.9 %copy.32 = bf16[1,1024,1024]{1,2,0:T(8,128)(2,1)} copy(bf16[1,1024,1024]{2,1,0:T(8,128)(2,1)} %constant_dynamic-slice_fusion) | data formatting | bytes 4194304
  66.9 39.1 %collective-permute-done = bf16[8,64,1024]{2,1,0:T(8,128)(2,1)} collective-permute-done((bf16[8,64,1024]{2,1,0:T(8,128)(2,1)S(1)}, bf16[8,64,1024]{2,1,0:T(8,128)(2,1)}, u32[]{:S(2)}, u32[]{:S(2)}) %collective-permute-start) | collective-permute-done | bytes 1048608 | tf_op jit(solution)/shard_map/ppermute | solution.py:10
  106.1 49.0 %all-to-all-done.1 = bf16[16,256,512]{2,0,1:T(8,128)(2,1)} async-done(((bf16[16,256,512]{2,0,1:T(8,128)(2,1)}), bf16[16,256,512]{2,0,1:T(8,128)(2,1)}, u32[]{:S(2)}, u32[]{:S(2)}) %all-to-all-start.1) | async-done | bytes 4194336 | tf_op jit(solution)/shard_map/all_to_all | solution.py:45
  155.1 10.4 %convolution_convert_fusion = bf16[2,128,16,1024]{3,1,2,0:T(8,128)(2,1)S(1)} fusion(bf16[1024,2,512,1]{0,2,3,1:T(8,128)(2,1)} %bitcast.42, bf16[128,2,16,512]{3,2,1,0:T(8,128)(2,1)} %bitcast.12), kind=kOutput, calls=%fused_computation.6 | convolution fusion | flops 4299161600 | bytes 14680064 | tf_op jit(solution)/shard_map/tric,arc->rtia/dot_general | solution.py:50
  165.5 2.1 add_convert_fusion
  167.6 1.0 subtract_convert_fusion
  168.6 0.0 copy-start.2
  168.6 2.9 %copy.27 = bf16[2,64,2,4,1024]{4,3,2,1,0:T(4,128)(2,1)} copy(bf16[2,64,2,4,1024]{4,1,3,0,2:T(8,128)(2,1)S(1)} %bitcast.40) | data formatting | bytes 4194304 | tf_op jit(solution)/shard_map/transpose | solution.py:60
  171.5 7.1 %all-to-all-start.2 = ((bf16[256,4,1024]{2,1,0:T(4,128)(2,1)}), bf16[256,4,1024]{2,1,0:T(4,128)(2,1)}, u32[]{:S(2)}, u32[]{:S(2)}) async-start(bf16[256,4,1024]{2,1,0:T(4,128)(2,1)} %bitcast.41), calls=%async_computation.2 | async-start | bytes 4194304 | tf_op jit(solution)/shard_map/all_to_all | solution.py:62
  178.6 0.0 copy-done.2
  178.6 1.0 sort.35
  179.6 0.1 slice.57
  179.6 1.8 gather_fusion.2
  181.5 2.6 %gather_fusion.3 = bf16[4,64,1024]{2,1,0:T(8,128)(2,1)} fusion(bf16[8,64,1024]{2,1,0:T(8,128)(2,1)} %collective-permute-done, s32[1024]{0:T(1024)S(1)} %pad_clamp_fusion.1), kind=kCustom, calls=%fused_computation.3 | custom fusion | bytes 1048592 | tf_op jit(solution)/shard_map/jit(_take)/gather | solution.py:76
  184.1 46.9 %all-to-all-done.2 = bf16[256,4,1024]{2,1,0:T(4,128)(2,1)} async-done(((bf16[256,4,1024]{2,1,0:T(4,128)(2,1)}), bf16[256,4,1024]{2,1,0:T(4,128)(2,1)}, u32[]{:S(2)}, u32[]{:S(2)}) %all-to-all-start.2) | async-done | bytes 2097184 | tf_op jit(solution)/shard_map/all_to_all | solution.py:62
  231.0 3.0 %fusion.12 = bf16[4,64,1024]{2,1,0:T(8,128)(2,1)S(1)} fusion(bf16[256,4,1024]{2,1,0:T(4,128)(2,1)} %all-to-all-done.2, bf16[4,64,1024]{2,1,0:T(8,128)(2,1)S(1)} %gather_fusion.2, bf16[4,64,1024]{2,1,0:T(8,128)(2,1)} %gather_fusion.3, bf16[8,64,1024]{2,1,0:T(8,128)(2,1)} %param.13, bf16[8,64,1024]{2,1,0:T(8,128)(2,1)} %collective-permute-done, pred[]{:T(512)S(6)} %ge.3, ...), kind=kOutput, calls=%fused_computation.14 | convolution fusion | flops 136347648 | bytes 4719873 | tf_op jit(solution)/shard_map/qa,qrc->rac/dot_general | solution.py:68
  234.1 0.2 collective-permute-start.1
  234.2 14.3 %collective-permute-done.1 = bf16[4,64,1024]{2,1,0:T(8,128)(2,1)S(1)} collective-permute-done((bf16[4,64,1024]{2,1,0:T(8,128)(2,1)S(1)}, bf16[4,64,1024]{2,1,0:T(8,128)(2,1)S(1)}, u32[]{:S(2)}, u32[]{:S(2)}) %collective-permute-start.1) | collective-permute-done | bytes 524320 | tf_op jit(solution)/shard_map/ppermute | solution.py:10
  248.5 0.1 broadcast_select_fusion
  248.6 1.1 pad_maximum_fusion
  249.7 1.8 gather_fusion.4
  251.5 1.0 broadcast_multiply_fusion
  (14 shorter events, 0.1 us)
Async XLA Ops:
  0.0 38.1 %copy-start = (bf16[16,128,512]{2,1,0:T(8,128)(2,1)S(1)}, bf16[16,128,512]{2,1,0:T(8,128)(2,1)}, u32[]{:S(2)}) copy-start(bf16[16,128,512]{2,1,0:T(8,128)(2,1)} %param.7) | copy-start | bytes 6291460
  10.1 26.9 %all-to-all-start = ((s32[256,1,11]{2,1,0:T(1,128)}), s32[256,1,11]{2,1,0:T(1,128)S(1)}, u32[]{:S(2)}, u32[]{:S(2)}) async-start(s32[256,1,11]{2,1,0:T(1,128)} %broadcast_in_dim.30), calls=%async_computation | async-start | bytes 262144 | tf_op jit(solution)/shard_map/all_to_all | solution.py:34
  48.6 8.4 %copy-start.1 = (bf16[8,64,1024]{2,1,0:T(8,128)(2,1)S(1)}, bf16[8,64,1024]{2,1,0:T(8,128)(2,1)}, u32[]{:S(2)}) copy-start(bf16[8,64,1024]{2,1,0:T(8,128)(2,1)} %param.13) | copy-start | bytes 3145732
  48.6 106.5 %all-to-all-start.1 = ((bf16[16,256,512]{2,0,1:T(8,128)(2,1)}), bf16[16,256,512]{2,0,1:T(8,128)(2,1)}, u32[]{:S(2)}, u32[]{:S(2)}) async-start(bf16[16,256,512]{2,0,1:T(8,128)(2,1)} %bitcast.39), calls=%async_computation.1 | async-start | bytes 8388608 | tf_op jit(solution)/shard_map/all_to_all | solution.py:45
  57.0 49.1 %collective-permute-start = (bf16[8,64,1024]{2,1,0:T(8,128)(2,1)S(1)}, bf16[8,64,1024]{2,1,0:T(8,128)(2,1)}, u32[]{:S(2)}, u32[]{:S(2)}) collective-permute-start(bf16[8,64,1024]{2,1,0:T(8,128)(2,1)S(1)} %copy-done.1), channel_id=1, source_target_pairs={{0,128},{2,130},{4,132},{6,134},{8,136},{10,138},{12,140},{14,142}... | collective-permute-start | bytes 3145736 | tf_op jit(solution)/shard_map/ppermute | solution.py:10
  168.6 10.0 %copy-start.2 = (s32[8]{0:T(128)S(1)}, s32[8]{0:T(128)}, u32[]{:S(2)}) copy-start(s32[8]{0:T(128)} %param.12) | copy-start | bytes 100
  171.5 59.5 %all-to-all-start.2 = ((bf16[256,4,1024]{2,1,0:T(4,128)(2,1)}), bf16[256,4,1024]{2,1,0:T(4,128)(2,1)}, u32[]{:S(2)}, u32[]{:S(2)}) async-start(bf16[256,4,1024]{2,1,0:T(4,128)(2,1)} %bitcast.41), calls=%async_computation.2 | async-start | bytes 4194304 | tf_op jit(solution)/shard_map/all_to_all | solution.py:62
  234.1 14.5 %collective-permute-start.1 = (bf16[4,64,1024]{2,1,0:T(8,128)(2,1)S(1)}, bf16[4,64,1024]{2,1,0:T(8,128)(2,1)S(1)}, u32[]{:S(2)}, u32[]{:S(2)}) collective-permute-start(bf16[4,64,1024]{2,1,0:T(8,128)(2,1)S(1)} %fusion.12), channel_id=1, source_target_pairs={{0,128},{2,130},{4,132},{6,134},{8,136},{10,138},{12,140},{14,142}... | collective-permute-start | bytes 1572872 | tf_op jit(solution)/shard_map/ppermute | solution.py:10

commit v7 on v6

--- a/solution.py
+++ b/solution.py
@@ -40,7 +40,10 @@
     inverse_rows = (inverse_rows + local_rows * jnp.arange(blocks)[:, None]).reshape(-1)
     row_order = jnp.where(upper, inverse_rows, jnp.arange(rows_own))
 
-    by_row = jnp.take(amplitudes, row_order, axis=0, mode="clip")
+    reorder = (row_order[:, None] == jnp.arange(rows_own)[None, :]).astype(amplitudes.dtype)
+    by_row = jnp.einsum(
+        "ij,jdc->idc", reorder, amplitudes, preferred_element_type=jnp.float32
+    ).astype(amplitudes.dtype)
     outgoing = jnp.take(by_row, every_cd, axis=1, mode="clip")
     incoming = lax.all_to_all(outgoing, BOTH, split_axis=1, concat_axis=0, tiled=True)
     incoming = incoming.reshape(peer_count, rep_count, rows_own, half_cols)

time: 253 us -> 250 us (0.988)
  local copies, waits for them, and re-layouts: 28.3 us -> 22.2 us
  matrix products: 13.4 us -> 16.1 us
    gather x2 -> x0, local copies, waits for them, and re-layouts: 6.11 us -> none  [per_device(): by_row = jnp.take(amplitudes, row_order, axis=0, mode='clip')]
    dot_general x0 -> x1, matrix products: none -> 2.69 us  [per_device(): jnp.einsum('ij,jdc->idc', reorder, amplitudes, preferred_element_type=jnp...]
where the time goes in v7:
time: 250 us; the launch traced here: 249 us
  waiting for transfers between devices  162 us (65%)
  starting transfers between devices  33.3 us (13%)
  local copies, waits for them, and re-layouts  22.2 us (9%)
  matrix products  16.1 us (6%)
  other arithmetic  13.1 us (5%)
  between operations  2.79 us (1%)
    ppermute x2, waiting for transfers between devices, partner_2(): lax.ppermute(shard, axis, [(i, i ^ 1 << bit) for i in range(lax.axis_size...  53.4 us
    all_to_all x1, waiting for transfers between devices, per_device(): lax.all_to_all(outgoing, BOTH, split_axis=1, concat_axis=0, tiled=True)  49 us
    all_to_all x1, waiting for transfers between devices, per_device(): lax.all_to_all(pairs, BOTH, split_axis=0, concat_axis=0, tiled=True)  46.9 us
    all_to_all x1, starting transfers between devices, per_device(): every = lax.all_to_all(mine, BOTH, split_axis=0, concat_axis=0, tiled=True)  14.7 us
    all_to_all x1, waiting for transfers between devices, per_device(): every = lax.all_to_all(mine, BOTH, split_axis=0, concat_axis=0, tiled=True)  12.2 us
    dot_general x1, matrix products, per_device(): jnp.einsum('tric,arc->rtia', incoming, integral, preferred_element_type=j...  10.4 us
    all_to_all x1, starting transfers between devices, per_device(): lax.all_to_all(outgoing, BOTH, split_axis=1, concat_axis=0, tiled=True)  8.36 us
    all_to_all x1, starting transfers between devices, per_device(): lax.all_to_all(pairs, BOTH, split_axis=0, concat_axis=0, tiled=True)  7.07 us
  transfers between devices with their start and end apart: 5, of which 5 were waited for; matrix products, arithmetic and copies ran while one was open for 5% of the time, Pallas kernels for 0%

profile of v7, /device:TPU:33, one launch (start us, length us, event | category | flops | bytes accessed | tf_op | source)
XLA Modules:
  0.0 249.1 jit_solution(10758597482069695529)
XLA Ops:
  0.0 0.0 copy-start
  0.0 0.8 broadcast_compare_fusion
  0.8 0.7 fusion.31
  4.1 1.4 select_reduce_fusion
  5.5 1.3 select_reduce_fusion.2
  6.8 2.6 %pad_add_fusion = s32[11]{0:T(128)S(1)} fusion(s32[8]{0:T(128)} %param.12, s32[1]{0:T(128)} %bitcast.5, s32[1]{0:T(128)} %bitcast.4, s32[1]{0:T(128)} %bitcast.3), kind=kLoop, calls=%fused_computation.45 | loop fusion | flops 33 | bytes 88 | tf_op jit(solution)/shard_map/concatenate | solution.py:32
  9.4 0.7 broadcast_in_dim.30
  10.1 14.7 %all-to-all-start = ((s32[256,1,11]{2,1,0:T(1,128)}), s32[256,1,11]{2,1,0:T(1,128)S(1)}, u32[]{:S(2)}, u32[]{:S(2)}) async-start(s32[256,1,11]{2,1,0:T(1,128)} %broadcast_in_dim.30), calls=%async_computation | async-start | bytes 262144 | tf_op jit(solution)/shard_map/all_to_all | solution.py:34
  24.8 12.2 %all-to-all-done = s32[256,1,11]{2,1,0:T(1,128)S(1)} async-done(((s32[256,1,11]{2,1,0:T(1,128)}), s32[256,1,11]{2,1,0:T(1,128)S(1)}, u32[]{:S(2)}, u32[]{:S(2)}) %all-to-all-start) | async-done | bytes 11296 | tf_op jit(solution)/shard_map/all_to_all | solution.py:34
  37.1 0.1 copy.17
  37.2 0.1 add_select_fusion
  37.3 0.7 sort.34
  37.9 0.1 copy.18
  38.0 0.1 reshape.52
  38.1 0.0 copy-done
  38.1 2.7 %fusion.5 = bf16[16,128,512]{2,0,1:T(8,128)(2,1)} fusion(bf16[16,128,512]{2,1,0:T(8,128)(2,1)S(1)} %copy-done, s32[16]{0:T(128)S(1)} %broadcast_select_fusion.3), kind=kOutput, calls=%fused_computation.12 | convolution fusion | flops 34603264 | bytes 4194368 | tf_op jit(solution)/shard_map/ij,jdc->idc/dot_general | solution.py:44
  40.8 4.3 %gather_fusion = bf16[256,16,512]{2,1,0:T(8,128)(2,1)} fusion(bf16[16,128,512]{2,0,1:T(8,128)(2,1)} %fusion.5, s32[1024]{0:T(1024)S(1)} %pad_clamp_fusion.3), kind=kCustom, calls=%fused_computation | custom fusion | bytes 8389632 | tf_op jit(solution)/shard_map/jit(_take)/gather | solution.py:47
  45.1 0.0 copy-start.1
  45.1 8.4 %all-to-all-start.1 = ((bf16[16,256,512]{2,0,1:T(8,128)(2,1)}), bf16[16,256,512]{2,0,1:T(8,128)(2,1)}, u32[]{:S(2)}, u32[]{:S(2)}) async-start(bf16[16,256,512]{2,0,1:T(8,128)(2,1)} %bitcast.40), calls=%async_computation.1 | async-start | bytes 8388608 | tf_op jit(solution)/shard_map/all_to_all | solution.py:48
  53.5 0.0 copy-done.1
  53.5 3.0 %collective-permute-start = (bf16[8,64,1024]{2,1,0:T(8,128)(2,1)S(1)}, bf16[8,64,1024]{2,1,0:T(8,128)(2,1)}, u32[]{:S(2)}, u32[]{:S(2)}) collective-permute-start(bf16[8,64,1024]{2,1,0:T(8,128)(2,1)S(1)} %copy-done.1), channel_id=1, source_target_pairs={{0,128},{2,130},{4,132},{6,134},{8,136},{10,138},{12,140},{14,142}... | collective-permute-start | bytes 3145736 | tf_op jit(solution)/shard_map/ppermute | solution.py:10
  56.5 3.1 %constant_dynamic-slice_fusion = bf16[1,1024,1024]{2,1,0:T(8,128)(2,1)} fusion(bf16[3,1024,1024]{2,1,0:T(8,128)(2,1)} %param.8, s32[]{:T(128)S(6)} %select_n.117), kind=kLoop, calls=%fused_computation.50 | loop fusion | bytes 4194308 | tf_op jit(solution)/shard_map/jit(dynamic_index_in_dim)/dynamic_slice | solution.py:51
  59.6 3.9 %copy.28 = bf16[1,1024,1024]{1,2,0:T(8,128)(2,1)} copy(bf16[1,1024,1024]{2,1,0:T(8,128)(2,1)} %constant_dynamic-slice_fusion) | data formatting | bytes 4194304
  63.5 39.1 %collective-permute-done = bf16[8,64,1024]{2,1,0:T(8,128)(2,1)} collective-permute-done((bf16[8,64,1024]{2,1,0:T(8,128)(2,1)S(1)}, bf16[8,64,1024]{2,1,0:T(8,128)(2,1)}, u32[]{:S(2)}, u32[]{:S(2)}) %collective-permute-start) | collective-permute-done | bytes 1048608 | tf_op jit(solution)/shard_map/ppermute | solution.py:10
  102.6 49.0 %all-to-all-done.1 = bf16[16,256,512]{2,0,1:T(8,128)(2,1)} async-done(((bf16[16,256,512]{2,0,1:T(8,128)(2,1)}), bf16[16,256,512]{2,0,1:T(8,128)(2,1)}, u32[]{:S(2)}, u32[]{:S(2)}) %all-to-all-start.1) | async-done | bytes 4194336 | tf_op jit(solution)/shard_map/all_to_all | solution.py:48
  151.6 10.4 %convolution_convert_fusion = bf16[2,128,16,1024]{3,1,2,0:T(8,128)(2,1)S(1)} fusion(bf16[1024,2,512,1]{0,2,3,1:T(8,128)(2,1)} %bitcast.43, bf16[128,2,16,512]{3,2,1,0:T(8,128)(2,1)} %bitcast.12), kind=kOutput, calls=%fused_computation.5 | convolution fusion | flops 4299161600 | bytes 14680064 | tf_op jit(solution)/shard_map/tric,arc->rtia/dot_general | solution.py:53
  162.1 2.1 add_convert_fusion
  164.1 1.0 subtract_convert_fusion
  165.1 0.0 copy-start.2
  165.1 2.9 %copy.23 = bf16[2,64,2,4,1024]{4,3,2,1,0:T(4,128)(2,1)} copy(bf16[2,64,2,4,1024]{4,1,3,0,2:T(8,128)(2,1)S(1)} %bitcast.41) | data formatting | bytes 4194304 | tf_op jit(solution)/shard_map/transpose | solution.py:63
  168.1 7.1 %all-to-all-start.2 = ((bf16[256,4,1024]{2,1,0:T(4,128)(2,1)}), bf16[256,4,1024]{2,1,0:T(4,128)(2,1)}, u32[]{:S(2)}, u32[]{:S(2)}) async-start(bf16[256,4,1024]{2,1,0:T(4,128)(2,1)} %bitcast.42), calls=%async_computation.2 | async-start | bytes 4194304 | tf_op jit(solution)/shard_map/all_to_all | solution.py:65
  175.1 0.0 copy-done.2
  175.2 1.0 sort.35
  176.1 0.1 slice.57
  176.2 1.8 gather_fusion.1
  178.1 2.6 %gather_fusion.2 = bf16[4,64,1024]{2,1,0:T(8,128)(2,1)} fusion(bf16[8,64,1024]{2,1,0:T(8,128)(2,1)} %collective-permute-done, s32[1024]{0:T(1024)S(1)} %pad_clamp_fusion.1), kind=kCustom, calls=%fused_computation.2 | custom fusion | bytes 1048592 | tf_op jit(solution)/shard_map/jit(_take)/gather | solution.py:79
  180.7 46.9 %all-to-all-done.2 = bf16[256,4,1024]{2,1,0:T(4,128)(2,1)} async-done(((bf16[256,4,1024]{2,1,0:T(4,128)(2,1)}), bf16[256,4,1024]{2,1,0:T(4,128)(2,1)}, u32[]{:S(2)}, u32[]{:S(2)}) %all-to-all-start.2) | async-done | bytes 2097184 | tf_op jit(solution)/shard_map/all_to_all | solution.py:65
  227.6 3.0 %fusion.17 = bf16[4,64,1024]{2,1,0:T(8,128)(2,1)S(1)} fusion(bf16[256,4,1024]{2,1,0:T(4,128)(2,1)} %all-to-all-done.2, bf16[4,64,1024]{2,1,0:T(8,128)(2,1)S(1)} %gather_fusion.1, bf16[4,64,1024]{2,1,0:T(8,128)(2,1)} %gather_fusion.2, bf16[8,64,1024]{2,1,0:T(8,128)(2,1)} %param.13, bf16[8,64,1024]{2,1,0:T(8,128)(2,1)} %collective-permute-done, pred[]{:T(512)S(6)} %ge.3, ...), kind=kOutput, calls=%fused_computation.16 | convolution fusion | flops 136347648 | bytes 4719873 | tf_op jit(solution)/shard_map/qa,qrc->rac/dot_general | solution.py:71
  230.6 0.2 collective-permute-start.1
  230.8 14.3 %collective-permute-done.1 = bf16[4,64,1024]{2,1,0:T(8,128)(2,1)S(1)} collective-permute-done((bf16[4,64,1024]{2,1,0:T(8,128)(2,1)S(1)}, bf16[4,64,1024]{2,1,0:T(8,128)(2,1)S(1)}, u32[]{:S(2)}, u32[]{:S(2)}) %collective-permute-start.1) | collective-permute-done | bytes 524320 | tf_op jit(solution)/shard_map/ppermute | solution.py:10
  245.1 0.1 broadcast_select_fusion
  245.2 1.1 pad_maximum_fusion
  246.2 1.8 gather_fusion.3
  248.1 1.0 broadcast_multiply_fusion
  (13 shorter events, 0.1 us)
Async XLA Ops:
  0.0 38.1 %copy-start = (bf16[16,128,512]{2,1,0:T(8,128)(2,1)S(1)}, bf16[16,128,512]{2,1,0:T(8,128)(2,1)}, u32[]{:S(2)}) copy-start(bf16[16,128,512]{2,1,0:T(8,128)(2,1)} %param.7) | copy-start | bytes 6291460
  10.1 26.9 %all-to-all-start = ((s32[256,1,11]{2,1,0:T(1,128)}), s32[256,1,11]{2,1,0:T(1,128)S(1)}, u32[]{:S(2)}, u32[]{:S(2)}) async-start(s32[256,1,11]{2,1,0:T(1,128)} %broadcast_in_dim.30), calls=%async_computation | async-start | bytes 262144 | tf_op jit(solution)/shard_map/all_to_all | solution.py:34
  45.1 8.4 %copy-start.1 = (bf16[8,64,1024]{2,1,0:T(8,128)(2,1)S(1)}, bf16[8,64,1024]{2,1,0:T(8,128)(2,1)}, u32[]{:S(2)}) copy-start(bf16[8,64,1024]{2,1,0:T(8,128)(2,1)} %param.13) | copy-start | bytes 3145732
  45.1 106.5 %all-to-all-start.1 = ((bf16[16,256,512]{2,0,1:T(8,128)(2,1)}), bf16[16,256,512]{2,0,1:T(8,128)(2,1)}, u32[]{:S(2)}, u32[]{:S(2)}) async-start(bf16[16,256,512]{2,0,1:T(8,128)(2,1)} %bitcast.40), calls=%async_computation.1 | async-start | bytes 8388608 | tf_op jit(solution)/shard_map/all_to_all | solution.py:48
  53.5 49.1 %collective-permute-start = (bf16[8,64,1024]{2,1,0:T(8,128)(2,1)S(1)}, bf16[8,64,1024]{2,1,0:T(8,128)(2,1)}, u32[]{:S(2)}, u32[]{:S(2)}) collective-permute-start(bf16[8,64,1024]{2,1,0:T(8,128)(2,1)S(1)} %copy-done.1), channel_id=1, source_target_pairs={{0,128},{2,130},{4,132},{6,134},{8,136},{10,138},{12,140},{14,142}... | collective-permute-start | bytes 3145736 | tf_op jit(solution)/shard_map/ppermute | solution.py:10
  165.1 10.0 %copy-start.2 = (s32[8]{0:T(128)S(1)}, s32[8]{0:T(128)}, u32[]{:S(2)}) copy-start(s32[8]{0:T(128)} %param.12) | copy-start | bytes 100
  168.1 59.5 %all-to-all-start.2 = ((bf16[256,4,1024]{2,1,0:T(4,128)(2,1)}), bf16[256,4,1024]{2,1,0:T(4,128)(2,1)}, u32[]{:S(2)}, u32[]{:S(2)}) async-start(bf16[256,4,1024]{2,1,0:T(4,128)(2,1)} %bitcast.42), calls=%async_computation.2 | async-start | bytes 4194304 | tf_op jit(solution)/shard_map/all_to_all | solution.py:65
  230.6 14.5 %collective-permute-start.1 = (bf16[4,64,1024]{2,1,0:T(8,128)(2,1)S(1)}, bf16[4,64,1024]{2,1,0:T(8,128)(2,1)S(1)}, u32[]{:S(2)}, u32[]{:S(2)}) collective-permute-start(bf16[4,64,1024]{2,1,0:T(8,128)(2,1)S(1)} %fusion.17), channel_id=1, source_target_pairs={{0,128},{2,130},{4,132},{6,134},{8,136},{10,138},{12,140},{14,142}... | collective-permute-start | bytes 1572872 | tf_op jit(solution)/shard_map/ppermute | solution.py:10

commit v8 on v7

--- a/solution.py
+++ b/solution.py
@@ -29,10 +29,13 @@
     slot = jnp.where(rep == 0, first, second)
     pick = jnp.arange(task_cd.shape[0]) == slot
     chosen = [jnp.sum(jnp.where(pick, ids, 0)) for ids in (task_cd, task_ab, task_allowed)]
-    mine = jnp.concatenate([jnp.stack(chosen), mirror])
-    mine = jnp.broadcast_to(mine[None], (peer_count * rep_count, mine.shape[0]))
+    pair_span = 2 * peer_count * rep_count * local_rows
+    code = chosen[0] + 256 * (chosen[1] + 256 * chosen[2])
+    mine = jnp.broadcast_to((mirror + pair_span * code)[None], (peer_count * rep_count, local_rows))
     every = lax.all_to_all(mine, BOTH, split_axis=0, concat_axis=0, tiled=True)
-    every_cd, every_ab, every_allowed = every[:, 0], every[:, 1], every[:, 2]
+    packed = every[:, 0] // pair_span
+    every_cd, every_ab, every_allowed = packed % 256, packed // 256 % 256, packed // 65536
+    every = jnp.concatenate([jnp.zeros((every.shape[0], 3), every.dtype), every % pair_span], axis=1)
 
     blocks = rows_own // local_rows
     own_blocks = lax.dynamic_slice_in_dim(every[:, 3:], lax.axis_index("tile") * blocks, blocks)

time: 250 us -> 250 us (level)
    concatenate x1 -> x0, other arithmetic: 2.62 us -> none  [per_device(): mine = jnp.concatenate([jnp.stack(chosen), mirror])]
where the time goes in v8:
time: 250 us; the launch traced here: 249 us
  waiting for transfers between devices  162 us (65%)
  starting transfers between devices  33.3 us (13%)
  local copies, waits for them, and re-layouts  22.2 us (9%)
  matrix products  16.1 us (6%)
  other arithmetic  11.2 us (4%)
  between operations  4.78 us (2%)
    ppermute x2, waiting for transfers between devices, partner_2(): lax.ppermute(shard, axis, [(i, i ^ 1 << bit) for i in range(lax.axis_size...  53.4 us
    all_to_all x1, waiting for transfers between devices, per_device(): lax.all_to_all(outgoing, BOTH, split_axis=1, concat_axis=0, tiled=True)  49 us
    all_to_all x1, waiting for transfers between devices, per_device(): lax.all_to_all(pairs, BOTH, split_axis=0, concat_axis=0, tiled=True)  47 us
    all_to_all x1, starting transfers between devices, per_device(): every = lax.all_to_all(mine, BOTH, split_axis=0, concat_axis=0, tiled=True)  14.7 us
    all_to_all x1, waiting for transfers between devices, per_device(): every = lax.all_to_all(mine, BOTH, split_axis=0, concat_axis=0, tiled=True)  12.2 us
    dot_general x1, matrix products, per_device(): jnp.einsum('tric,arc->rtia', incoming, integral, preferred_element_type=j...  10.4 us
    all_to_all x1, starting transfers between devices, per_device(): lax.all_to_all(outgoing, BOTH, split_axis=1, concat_axis=0, tiled=True)  8.36 us
    all_to_all x1, starting transfers between devices, per_device(): lax.all_to_all(pairs, BOTH, split_axis=0, concat_axis=0, tiled=True)  7.07 us
  transfers between devices with their start and end apart: 5, of which 5 were waited for; matrix products, arithmetic and copies ran while one was open for 5% of the time, Pallas kernels for 0%

profile of v8, /device:TPU:33, one launch (start us, length us, event | category | flops | bytes accessed | tf_op | source)
XLA Modules:
  0.0 249.2 jit_solution(8864760171226509197)
XLA Ops:
  0.0 0.0 copy-start
  0.0 0.8 broadcast_compare_fusion.2
  0.8 0.7 fusion.31
  4.1 1.4 select_reduce_fusion
  6.8 1.3 select_reduce_fusion.2
  8.8 0.7 broadcast_select_fusion.2
  9.5 0.7 broadcast_in_dim.32
  10.2 14.7 %all-to-all-start = ((s32[256,1,8]{2,1,0:T(1,128)}), s32[256,1,8]{2,1,0:T(1,128)S(1)}, u32[]{:S(2)}, u32[]{:S(2)}) async-start(s32[256,1,8]{2,1,0:T(1,128)} %broadcast_in_dim.32), calls=%async_computation | async-start | bytes 262144 | tf_op jit(solution)/shard_map/all_to_all | solution.py:35
  24.9 12.2 %all-to-all-done = s32[256,1,8]{2,1,0:T(1,128)S(1)} async-done(((s32[256,1,8]{2,1,0:T(1,128)}), s32[256,1,8]{2,1,0:T(1,128)S(1)}, u32[]{:S(2)}, u32[]{:S(2)}) %all-to-all-start) | async-done | bytes 8224 | tf_op jit(solution)/shard_map/all_to_all | solution.py:35
  37.1 0.1 copy.17
  37.2 0.1 add_select_fusion
  37.3 0.7 sort.34
  38.0 0.1 copy.18
  38.0 0.1 reshape.53
  38.2 0.0 copy-done
  38.2 2.7 %fusion.5 = bf16[16,128,512]{2,0,1:T(8,128)(2,1)} fusion(bf16[16,128,512]{2,1,0:T(8,128)(2,1)S(1)} %copy-done, s32[16]{0:T(128)S(1)} %broadcast_select_fusion.3), kind=kOutput, calls=%fused_computation.12 | convolution fusion | flops 34603264 | bytes 4194368 | tf_op jit(solution)/shard_map/ij,jdc->idc/dot_general | solution.py:47
  40.9 4.3 %gather_fusion = bf16[256,16,512]{2,1,0:T(8,128)(2,1)} fusion(bf16[16,128,512]{2,0,1:T(8,128)(2,1)} %fusion.5, s32[1024]{0:T(1024)S(1)} %pad_clamp_fusion.3), kind=kCustom, calls=%fused_computation | custom fusion | bytes 8389632 | tf_op jit(solution)/shard_map/jit(_take)/gather | solution.py:50
  45.3 0.0 copy-start.1
  45.3 8.4 %all-to-all-start.1 = ((bf16[16,256,512]{2,0,1:T(8,128)(2,1)}), bf16[16,256,512]{2,0,1:T(8,128)(2,1)}, u32[]{:S(2)}, u32[]{:S(2)}) async-start(bf16[16,256,512]{2,0,1:T(8,128)(2,1)} %bitcast.39), calls=%async_computation.1 | async-start | bytes 8388608 | tf_op jit(solution)/shard_map/all_to_all | solution.py:51
  53.6 0.0 copy-done.1
  53.6 3.0 %collective-permute-start = (bf16[8,64,1024]{2,1,0:T(8,128)(2,1)S(1)}, bf16[8,64,1024]{2,1,0:T(8,128)(2,1)}, u32[]{:S(2)}, u32[]{:S(2)}) collective-permute-start(bf16[8,64,1024]{2,1,0:T(8,128)(2,1)S(1)} %copy-done.1), channel_id=1, source_target_pairs={{0,128},{2,130},{4,132},{6,134},{8,136},{10,138},{12,140},{14,142}... | collective-permute-start | bytes 3145736 | tf_op jit(solution)/shard_map/ppermute | solution.py:10
  56.6 3.1 %constant_dynamic-slice_fusion = bf16[1,1024,1024]{2,1,0:T(8,128)(2,1)} fusion(bf16[3,1024,1024]{2,1,0:T(8,128)(2,1)} %param.8, s32[]{:T(128)S(6)} %select_n.154), kind=kLoop, calls=%fused_computation.65 | loop fusion | bytes 4194308 | tf_op jit(solution)/shard_map/jit(dynamic_index_in_dim)/dynamic_slice | solution.py:54
  59.7 3.9 %copy.28 = bf16[1,1024,1024]{1,2,0:T(8,128)(2,1)} copy(bf16[1,1024,1024]{2,1,0:T(8,128)(2,1)} %constant_dynamic-slice_fusion) | data formatting | bytes 4194304
  63.6 39.1 %collective-permute-done = bf16[8,64,1024]{2,1,0:T(8,128)(2,1)} collective-permute-done((bf16[8,64,1024]{2,1,0:T(8,128)(2,1)S(1)}, bf16[8,64,1024]{2,1,0:T(8,128)(2,1)}, u32[]{:S(2)}, u32[]{:S(2)}) %collective-permute-start) | collective-permute-done | bytes 1048608 | tf_op jit(solution)/shard_map/ppermute | solution.py:10
  102.7 49.0 %all-to-all-done.1 = bf16[16,256,512]{2,0,1:T(8,128)(2,1)} async-done(((bf16[16,256,512]{2,0,1:T(8,128)(2,1)}), bf16[16,256,512]{2,0,1:T(8,128)(2,1)}, u32[]{:S(2)}, u32[]{:S(2)}) %all-to-all-start.1) | async-done | bytes 4194336 | tf_op jit(solution)/shard_map/all_to_all | solution.py:51
  151.7 10.4 %convolution_convert_fusion = bf16[2,128,16,1024]{3,1,2,0:T(8,128)(2,1)S(1)} fusion(bf16[1024,2,512,1]{0,2,3,1:T(8,128)(2,1)} %bitcast.42, bf16[128,2,16,512]{3,2,1,0:T(8,128)(2,1)} %bitcast.9), kind=kOutput, calls=%fused_computation.5 | convolution fusion | flops 4299161600 | bytes 14680064 | tf_op jit(solution)/shard_map/tric,arc->rtia/dot_general | solution.py:56
  162.2 2.1 add_convert_fusion
  164.2 1.0 subtract_convert_fusion
  165.2 2.9 %copy.23 = bf16[2,64,2,4,1024]{4,3,2,1,0:T(4,128)(2,1)} copy(bf16[2,64,2,4,1024]{4,1,3,0,2:T(8,128)(2,1)S(1)} %bitcast.40) | data formatting | bytes 4194304 | tf_op jit(solution)/shard_map/transpose | solution.py:66
  168.2 7.1 %all-to-all-start.2 = ((bf16[256,4,1024]{2,1,0:T(4,128)(2,1)}), bf16[256,4,1024]{2,1,0:T(4,128)(2,1)}, u32[]{:S(2)}, u32[]{:S(2)}) async-start(bf16[256,4,1024]{2,1,0:T(4,128)(2,1)} %bitcast.41), calls=%async_computation.2 | async-start | bytes 4194304 | tf_op jit(solution)/shard_map/all_to_all | solution.py:68
  175.2 1.0 sort.35
  176.2 0.1 slice.47
  176.3 1.8 gather_fusion.1
  178.1 2.6 %gather_fusion.2 = bf16[4,64,1024]{2,1,0:T(8,128)(2,1)} fusion(bf16[8,64,1024]{2,1,0:T(8,128)(2,1)} %collective-permute-done, s32[1024]{0:T(1024)S(1)} %pad_clamp_fusion.1), kind=kCustom, calls=%fused_computation.2 | custom fusion | bytes 1048592 | tf_op jit(solution)/shard_map/jit(_take)/gather | solution.py:82
  180.7 47.0 %all-to-all-done.2 = bf16[256,4,1024]{2,1,0:T(4,128)(2,1)} async-done(((bf16[256,4,1024]{2,1,0:T(4,128)(2,1)}), bf16[256,4,1024]{2,1,0:T(4,128)(2,1)}, u32[]{:S(2)}, u32[]{:S(2)}) %all-to-all-start.2) | async-done | bytes 2097184 | tf_op jit(solution)/shard_map/all_to_all | solution.py:68
  227.7 3.0 %fusion.17 = bf16[4,64,1024]{2,1,0:T(8,128)(2,1)S(1)} fusion(bf16[256,4,1024]{2,1,0:T(4,128)(2,1)} %all-to-all-done.2, bf16[4,64,1024]{2,1,0:T(8,128)(2,1)S(1)} %gather_fusion.1, bf16[4,64,1024]{2,1,0:T(8,128)(2,1)} %gather_fusion.2, bf16[8,64,1024]{2,1,0:T(8,128)(2,1)} %param.13, bf16[8,64,1024]{2,1,0:T(8,128)(2,1)} %collective-permute-done, pred[]{:T(512)S(6)} %ge.3, ...), kind=kOutput, calls=%fused_computation.16 | convolution fusion | flops 136347648 | bytes 4719873 | tf_op jit(solution)/shard_map/qa,qrc->rac/dot_general | solution.py:74
  230.7 0.2 collective-permute-start.1
  230.9 14.3 %collective-permute-done.1 = bf16[4,64,1024]{2,1,0:T(8,128)(2,1)S(1)} collective-permute-done((bf16[4,64,1024]{2,1,0:T(8,128)(2,1)S(1)}, bf16[4,64,1024]{2,1,0:T(8,128)(2,1)S(1)}, u32[]{:S(2)}, u32[]{:S(2)}) %collective-permute-start.1) | collective-permute-done | bytes 524320 | tf_op jit(solution)/shard_map/ppermute | solution.py:10
  245.2 0.1 broadcast_select_fusion
  245.2 1.1 pad_maximum_fusion
  246.3 1.8 gather_fusion.3
  248.2 1.0 broadcast_multiply_fusion
  (14 shorter events, 0.1 us)
Async XLA Ops:
  0.0 38.2 %copy-start = (bf16[16,128,512]{2,1,0:T(8,128)(2,1)S(1)}, bf16[16,128,512]{2,1,0:T(8,128)(2,1)}, u32[]{:S(2)}) copy-start(bf16[16,128,512]{2,1,0:T(8,128)(2,1)} %param.7) | copy-start | bytes 6291460
  10.2 26.9 %all-to-all-start = ((s32[256,1,8]{2,1,0:T(1,128)}), s32[256,1,8]{2,1,0:T(1,128)S(1)}, u32[]{:S(2)}, u32[]{:S(2)}) async-start(s32[256,1,8]{2,1,0:T(1,128)} %broadcast_in_dim.32), calls=%async_computation | async-start | bytes 262144 | tf_op jit(solution)/shard_map/all_to_all | solution.py:35
  45.3 8.4 %copy-start.1 = (bf16[8,64,1024]{2,1,0:T(8,128)(2,1)S(1)}, bf16[8,64,1024]{2,1,0:T(8,128)(2,1)}, u32[]{:S(2)}) copy-start(bf16[8,64,1024]{2,1,0:T(8,128)(2,1)} %param.13) | copy-start | bytes 3145732
  45.3 106.5 %all-to-all-start.1 = ((bf16[16,256,512]{2,0,1:T(8,128)(2,1)}), bf16[16,256,512]{2,0,1:T(8,128)(2,1)}, u32[]{:S(2)}, u32[]{:S(2)}) async-start(bf16[16,256,512]{2,0,1:T(8,128)(2,1)} %bitcast.39), calls=%async_computation.1 | async-start | bytes 8388608 | tf_op jit(solution)/shard_map/all_to_all | solution.py:51
  53.6 49.1 %collective-permute-start = (bf16[8,64,1024]{2,1,0:T(8,128)(2,1)S(1)}, bf16[8,64,1024]{2,1,0:T(8,128)(2,1)}, u32[]{:S(2)}, u32[]{:S(2)}) collective-permute-start(bf16[8,64,1024]{2,1,0:T(8,128)(2,1)S(1)} %copy-done.1), channel_id=1, source_target_pairs={{0,128},{2,130},{4,132},{6,134},{8,136},{10,138},{12,140},{14,142}... | collective-permute-start | bytes 3145736 | tf_op jit(solution)/shard_map/ppermute | solution.py:10
  168.2 59.5 %all-to-all-start.2 = ((bf16[256,4,1024]{2,1,0:T(4,128)(2,1)}), bf16[256,4,1024]{2,1,0:T(4,128)(2,1)}, u32[]{:S(2)}, u32[]{:S(2)}) async-start(bf16[256,4,1024]{2,1,0:T(4,128)(2,1)} %bitcast.41), calls=%async_computation.2 | async-start | bytes 4194304 | tf_op jit(solution)/shard_map/all_to_all | solution.py:68
  230.7 14.5 %collective-permute-start.1 = (bf16[4,64,1024]{2,1,0:T(8,128)(2,1)S(1)}, bf16[4,64,1024]{2,1,0:T(8,128)(2,1)S(1)}, u32[]{:S(2)}, u32[]{:S(2)}) collective-permute-start(bf16[4,64,1024]{2,1,0:T(8,128)(2,1)S(1)} %fusion.17), channel_id=1, source_target_pairs={{0,128},{2,130},{4,132},{6,134},{8,136},{10,138},{12,140},{14,142}... | collective-permute-start | bytes 1572872 | tf_op jit(solution)/shard_map/ppermute | solution.py:10

commit v9 on v7

--- a/solution.py
+++ b/solution.py
@@ -61,8 +61,10 @@
     pairs = contribution.reshape(2, peer_count // 2, blocks, 2, quarter, tile_width)
     pairs = pairs[0].astype(jnp.float32) - pairs[1].astype(jnp.float32)
     pairs = pairs.astype(jnp.bfloat16).transpose(2, 0, 1, 3, 4)
-    pairs = pairs.reshape(peer_count * rep_count, quarter, tile_width)
+    chunk_rows = 16
+    pairs = pairs.reshape(peer_count * rep_count, chunk_rows, quarter * tile_width // chunk_rows)
     arrived = lax.all_to_all(pairs, BOTH, split_axis=0, concat_axis=0, tiled=True)
+    arrived = arrived.reshape(peer_count * rep_count, quarter, tile_width)
 
     tile_ids = jnp.arange(residual_in.shape[1], dtype=jnp.int32)
     weights = ((every_ab[:, None] == tile_ids[None, :]) & (every_allowed[:, None] == 1)).astype(

time: 250 us -> 258 us (1.032)
  local copies, waits for them, and re-layouts: 22.2 us -> 31 us
    reshape x0 -> x1, local copies, waits for them, and re-layouts: none -> 4.4 us  [per_device(): pairs.reshape(peer_count * rep_count, chunk_rows, quarter * tile_width //...]
    all_to_all x0 -> x1, local copies, waits for them, and re-layouts: none -> 4.28 us  [per_device(): lax.all_to_all(pairs, BOTH, split_axis=0, concat_axis=0, tiled=True)]
    convert_element_type x0 -> x1, local copies, waits for them, and re-layouts: none -> 2.98 us  [per_device(): pairs = pairs.astype(jnp.bfloat16).transpose(2, 0, 1, 3, 4)]
    transpose x1 -> x0, local copies, waits for them, and re-layouts: 2.92 us -> none  [per_device(): pairs = pairs.astype(jnp.bfloat16).transpose(2, 0, 1, 3, 4)]
where the time goes in v9:
time: 258 us
  waiting for transfers between devices  162 us (63%)
  starting transfers between devices  33.3 us (13%)
  local copies, waits for them, and re-layouts  31 us (12%)
  matrix products  15.9 us (6%)
  other arithmetic  13.1 us (5%)
  between operations  2.78 us (1%)
    ppermute x2, waiting for transfers between devices, partner_2(): lax.ppermute(shard, axis, [(i, i ^ 1 << bit) for i in range(lax.axis_size...  53.4 us
    all_to_all x1, waiting for transfers between devices, per_device(): lax.all_to_all(outgoing, BOTH, split_axis=1, concat_axis=0, tiled=True)  49 us
    all_to_all x1, waiting for transfers between devices, per_device(): lax.all_to_all(pairs, BOTH, split_axis=0, concat_axis=0, tiled=True)  46.9 us
    all_to_all x1, starting transfers between devices, per_device(): every = lax.all_to_all(mine, BOTH, split_axis=0, concat_axis=0, tiled=True)  14.7 us
    all_to_all x1, waiting for transfers between devices, per_device(): every = lax.all_to_all(mine, BOTH, split_axis=0, concat_axis=0, tiled=True)  12.2 us
    dot_general x1, matrix products, per_device(): jnp.einsum('tric,arc->rtia', incoming, integral, preferred_element_type=j...  10.4 us
    all_to_all x1, starting transfers between devices, per_device(): lax.all_to_all(outgoing, BOTH, split_axis=1, concat_axis=0, tiled=True)  8.36 us
    all_to_all x1, starting transfers between devices, per_device(): lax.all_to_all(pairs, BOTH, split_axis=0, concat_axis=0, tiled=True)  7.07 us
  transfers between devices with their start and end apart: 5, of which 5 were waited for; matrix products, arithmetic and copies ran while one was open for 5% of the time, Pallas kernels for 0%

profile of v9, /device:TPU:33, one launch (start us, length us, event | category | flops | bytes accessed | tf_op | source)
XLA Modules:
  0.0 257.5 jit_solution(16091896565334553850)
XLA Ops:
  0.0 0.0 copy-start
  0.0 0.8 broadcast_compare_fusion
  0.8 0.7 fusion.20
  4.1 1.4 select_reduce_fusion
  5.5 1.3 select_reduce_fusion.2
  6.8 2.6 %pad_add_fusion = s32[11]{0:T(128)S(1)} fusion(s32[8]{0:T(128)} %param.12, s32[1]{0:T(128)} %bitcast.5, s32[1]{0:T(128)} %bitcast.4, s32[1]{0:T(128)} %bitcast.3), kind=kLoop, calls=%fused_computation.44 | loop fusion | flops 33 | bytes 88 | tf_op jit(solution)/shard_map/concatenate | solution.py:32
  9.4 0.7 broadcast_in_dim.30
  10.1 14.7 %all-to-all-start = ((s32[256,1,11]{2,1,0:T(1,128)}), s32[256,1,11]{2,1,0:T(1,128)S(1)}, u32[]{:S(2)}, u32[]{:S(2)}) async-start(s32[256,1,11]{2,1,0:T(1,128)} %broadcast_in_dim.30), calls=%async_computation | async-start | bytes 262144 | tf_op jit(solution)/shard_map/all_to_all | solution.py:34
  24.8 12.2 %all-to-all-done = s32[256,1,11]{2,1,0:T(1,128)S(1)} async-done(((s32[256,1,11]{2,1,0:T(1,128)}), s32[256,1,11]{2,1,0:T(1,128)S(1)}, u32[]{:S(2)}, u32[]{:S(2)}) %all-to-all-start) | async-done | bytes 11296 | tf_op jit(solution)/shard_map/all_to_all | solution.py:34
  37.1 0.1 copy.18
  37.2 0.1 add_select_fusion
  37.3 0.7 sort.34
  37.9 0.1 copy.19
  38.0 0.1 reshape.55
  38.1 0.0 copy-done
  38.1 2.7 %fusion.3 = bf16[16,128,512]{2,0,1:T(8,128)(2,1)} fusion(bf16[16,128,512]{2,1,0:T(8,128)(2,1)S(1)} %copy-done, s32[16]{0:T(128)S(1)} %broadcast_select_fusion.3), kind=kOutput, calls=%fused_computation.11 | convolution fusion | flops 34603264 | bytes 4194368 | tf_op jit(solution)/shard_map/ij,jdc->idc/dot_general | solution.py:44
  40.8 4.3 %gather_fusion = bf16[256,16,512]{2,1,0:T(8,128)(2,1)} fusion(bf16[16,128,512]{2,0,1:T(8,128)(2,1)} %fusion.3, s32[1024]{0:T(1024)S(1)} %pad_clamp_fusion.3), kind=kCustom, calls=%fused_computation | custom fusion | bytes 8389632 | tf_op jit(solution)/shard_map/jit(_take)/gather | solution.py:47
  45.1 0.0 copy-start.1
  45.1 8.4 %all-to-all-start.1 = ((bf16[16,256,512]{2,0,1:T(8,128)(2,1)}), bf16[16,256,512]{2,0,1:T(8,128)(2,1)}, u32[]{:S(2)}, u32[]{:S(2)}) async-start(bf16[16,256,512]{2,0,1:T(8,128)(2,1)} %bitcast.42), calls=%async_computation.1 | async-start | bytes 8388608 | tf_op jit(solution)/shard_map/all_to_all | solution.py:48
  53.5 0.0 copy-done.1
  53.5 3.0 %collective-permute-start = (bf16[8,64,1024]{2,1,0:T(8,128)(2,1)S(1)}, bf16[8,64,1024]{2,1,0:T(8,128)(2,1)}, u32[]{:S(2)}, u32[]{:S(2)}) collective-permute-start(bf16[8,64,1024]{2,1,0:T(8,128)(2,1)S(1)} %copy-done.1), channel_id=1, source_target_pairs={{0,128},{2,130},{4,132},{6,134},{8,136},{10,138},{12,140},{14,142}... | collective-permute-start | bytes 3145736 | tf_op jit(solution)/shard_map/ppermute | solution.py:10
  56.5 3.1 %constant_dynamic-slice_fusion = bf16[1,1024,1024]{2,1,0:T(8,128)(2,1)} fusion(bf16[3,1024,1024]{2,1,0:T(8,128)(2,1)} %param.8, s32[]{:T(128)S(6)} %select_n.117), kind=kLoop, calls=%fused_computation.49 | loop fusion | bytes 4194308 | tf_op jit(solution)/shard_map/jit(dynamic_index_in_dim)/dynamic_slice | solution.py:51
  59.6 3.9 %copy.31 = bf16[1,1024,1024]{1,2,0:T(8,128)(2,1)} copy(bf16[1,1024,1024]{2,1,0:T(8,128)(2,1)} %constant_dynamic-slice_fusion) | data formatting | bytes 4194304
  63.5 39.1 %collective-permute-done = bf16[8,64,1024]{2,1,0:T(8,128)(2,1)} collective-permute-done((bf16[8,64,1024]{2,1,0:T(8,128)(2,1)S(1)}, bf16[8,64,1024]{2,1,0:T(8,128)(2,1)}, u32[]{:S(2)}, u32[]{:S(2)}) %collective-permute-start) | collective-permute-done | bytes 1048608 | tf_op jit(solution)/shard_map/ppermute | solution.py:10
  102.6 49.0 %all-to-all-done.1 = bf16[16,256,512]{2,0,1:T(8,128)(2,1)} async-done(((bf16[16,256,512]{2,0,1:T(8,128)(2,1)}), bf16[16,256,512]{2,0,1:T(8,128)(2,1)}, u32[]{:S(2)}, u32[]{:S(2)}) %all-to-all-start.1) | async-done | bytes 4194336 | tf_op jit(solution)/shard_map/all_to_all | solution.py:48
  151.6 10.4 %convolution_convert_fusion = bf16[2,128,16,1024]{3,1,2,0:T(8,128)(2,1)S(1)} fusion(bf16[1024,2,512,1]{0,2,3,1:T(8,128)(2,1)} %bitcast.45, bf16[128,2,16,512]{3,2,1,0:T(8,128)(2,1)} %bitcast.12), kind=kOutput, calls=%fused_computation.5 | convolution fusion | flops 4299161600 | bytes 14680064 | tf_op jit(solution)/shard_map/tric,arc->rtia/dot_general | solution.py:53
  162.1 2.1 add_convert_fusion
  164.1 1.0 subtract_convert_fusion
  165.1 3.0 %copy.39 = bf16[64,2,2,4,1024]{4,3,1,0,2:T(4,128)(2,1)} copy(bf16[64,2,2,4,1024]{4,0,3,2,1:T(8,128)(2,1)S(1)} %bitcast.43) | data formatting | bytes 4194304 | tf_op jit(solution)/shard_map/convert_element_type | solution.py:63
  168.1 0.0 copy-start.2
  168.1 4.4 %reshape.58 = bf16[256,16,256]{2,1,0:T(8,128)(2,1)} reshape(bf16[2,64,2,4,1024]{4,3,2,1,0:T(4,128)(2,1)} %bitcast.44) | data formatting | bytes 4194304 | tf_op jit(solution)/shard_map/reshape | solution.py:65
  172.5 7.1 %all-to-all-start.2 = ((bf16[256,16,256]{2,1,0:T(8,128)(2,1)}), bf16[256,16,256]{2,1,0:T(8,128)(2,1)}, u32[]{:S(2)}, u32[]{:S(2)}) async-start(bf16[256,16,256]{2,1,0:T(8,128)(2,1)} %reshape.58), calls=%async_computation.2 | async-start | bytes 4194304 | tf_op jit(solution)/shard_map/all_to_all | solution.py:66
  179.6 0.0 copy-done.2
  179.6 1.0 sort.35
  180.6 0.1 slice.57
  180.7 1.8 gather_fusion.1
  182.5 2.6 %gather_fusion.2 = bf16[4,64,1024]{2,1,0:T(8,128)(2,1)} fusion(bf16[8,64,1024]{2,1,0:T(8,128)(2,1)} %collective-permute-done, s32[1024]{0:T(1024)S(1)} %pad_clamp_fusion.1), kind=kCustom, calls=%fused_computation.2 | custom fusion | bytes 1048592 | tf_op jit(solution)/shard_map/jit(_take)/gather | solution.py:81
  185.1 46.9 %all-to-all-done.2 = bf16[256,16,256]{2,1,0:T(8,128)(2,1)} async-done(((bf16[256,16,256]{2,1,0:T(8,128)(2,1)}), bf16[256,16,256]{2,1,0:T(8,128)(2,1)}, u32[]{:S(2)}, u32[]{:S(2)}) %all-to-all-start.2) | async-done | bytes 2097184 | tf_op jit(solution)/shard_map/all_to_all | solution.py:66
  232.0 4.3 %copy.25 = bf16[256,16,256]{0,2,1:T(8,128)(2,1)} copy(bf16[256,16,256]{2,1,0:T(8,128)(2,1)} %all-to-all-done.2) | data formatting | bytes 4194304 | tf_op jit(solution)/shard_map/all_to_all | solution.py:66
  236.3 2.7 %fusion.8 = bf16[4,64,1024]{2,1,0:T(8,128)(2,1)S(1)} fusion(bf16[256,4,1024]{0,2,1:T(8,128)(2,1)} %bitcast.46, bf16[4,64,1024]{2,1,0:T(8,128)(2,1)S(1)} %gather_fusion.1, bf16[4,64,1024]{2,1,0:T(8,128)(2,1)} %gather_fusion.2, bf16[8,64,1024]{2,1,0:T(8,128)(2,1)} %param.13, bf16[8,64,1024]{2,1,0:T(8,128)(2,1)} %collective-permute-done, pred[]{:T(512)S(6)} %ge.3, ...), kind=kOutput, calls=%fused_computation.15 | convolution fusion | flops 136347648 | bytes 4719873 | tf_op jit(solution)/shard_map/qa,qrc->rac/dot_general | solution.py:73
  239.1 0.2 collective-permute-start.1
  239.2 14.3 %collective-permute-done.1 = bf16[4,64,1024]{2,1,0:T(8,128)(2,1)S(1)} collective-permute-done((bf16[4,64,1024]{2,1,0:T(8,128)(2,1)S(1)}, bf16[4,64,1024]{2,1,0:T(8,128)(2,1)S(1)}, u32[]{:S(2)}, u32[]{:S(2)}) %collective-permute-start.1) | collective-permute-done | bytes 524320 | tf_op jit(solution)/shard_map/ppermute | solution.py:10
  253.5 0.1 broadcast_select_fusion
  253.6 1.1 pad_maximum_fusion
  254.7 1.8 gather_fusion.3
  256.5 1.0 broadcast_multiply_fusion
  (13 shorter events, 0.1 us)
Async XLA Ops:
  0.0 38.1 %copy-start = (bf16[16,128,512]{2,1,0:T(8,128)(2,1)S(1)}, bf16[16,128,512]{2,1,0:T(8,128)(2,1)}, u32[]{:S(2)}) copy-start(bf16[16,128,512]{2,1,0:T(8,128)(2,1)} %param.7) | copy-start | bytes 6291460
  10.1 26.9 %all-to-all-start = ((s32[256,1,11]{2,1,0:T(1,128)}), s32[256,1,11]{2,1,0:T(1,128)S(1)}, u32[]{:S(2)}, u32[]{:S(2)}) async-start(s32[256,1,11]{2,1,0:T(1,128)} %broadcast_in_dim.30), calls=%async_computation | async-start | bytes 262144 | tf_op jit(solution)/shard_map/all_to_all | solution.py:34
  45.1 8.4 %copy-start.1 = (bf16[8,64,1024]{2,1,0:T(8,128)(2,1)S(1)}, bf16[8,64,1024]{2,1,0:T(8,128)(2,1)}, u32[]{:S(2)}) copy-start(bf16[8,64,1024]{2,1,0:T(8,128)(2,1)} %param.13) | copy-start | bytes 3145732
  45.1 106.5 %all-to-all-start.1 = ((bf16[16,256,512]{2,0,1:T(8,128)(2,1)}), bf16[16,256,512]{2,0,1:T(8,128)(2,1)}, u32[]{:S(2)}, u32[]{:S(2)}) async-start(bf16[16,256,512]{2,0,1:T(8,128)(2,1)} %bitcast.42), calls=%async_computation.1 | async-start | bytes 8388608 | tf_op jit(solution)/shard_map/all_to_all | solution.py:48
  53.5 49.1 %collective-permute-start = (bf16[8,64,1024]{2,1,0:T(8,128)(2,1)S(1)}, bf16[8,64,1024]{2,1,0:T(8,128)(2,1)}, u32[]{:S(2)}, u32[]{:S(2)}) collective-permute-start(bf16[8,64,1024]{2,1,0:T(8,128)(2,1)S(1)} %copy-done.1), channel_id=1, source_target_pairs={{0,128},{2,130},{4,132},{6,134},{8,136},{10,138},{12,140},{14,142}... | collective-permute-start | bytes 3145736 | tf_op jit(solution)/shard_map/ppermute | solution.py:10
  168.1 11.5 %copy-start.2 = (s32[8]{0:T(128)S(1)}, s32[8]{0:T(128)}, u32[]{:S(2)}) copy-start(s32[8]{0:T(128)} %param.12) | copy-start | bytes 100
  172.5 59.5 %all-to-all-start.2 = ((bf16[256,16,256]{2,1,0:T(8,128)(2,1)}), bf16[256,16,256]{2,1,0:T(8,128)(2,1)}, u32[]{:S(2)}, u32[]{:S(2)}) async-start(bf16[256,16,256]{2,1,0:T(8,128)(2,1)} %reshape.58), calls=%async_computation.2 | async-start | bytes 4194304 | tf_op jit(solution)/shard_map/all_to_all | solution.py:66
  239.1 14.5 %collective-permute-start.1 = (bf16[4,64,1024]{2,1,0:T(8,128)(2,1)S(1)}, bf16[4,64,1024]{2,1,0:T(8,128)(2,1)S(1)}, u32[]{:S(2)}, u32[]{:S(2)}) collective-permute-start(bf16[4,64,1024]{2,1,0:T(8,128)(2,1)S(1)} %fusion.8), channel_id=1, source_target_pairs={{0,128},{2,130},{4,132},{6,134},{8,136},{10,138},{12,140},{14,142}... | collective-permute-start | bytes 1572872 | tf_op jit(solution)/shard_map/ppermute | solution.py:10
